TPU v7x, 512 devices: a whole 4x8x8 slice. The times are simulated.
512 devices in a mesh: ctx: 8 (over y), dp: 64 (over x, z, core).
Axes of the slice: x: 4, y: 8, z: 8, core: 2. Of those that a mesh axis runs over, the one named last changes fastest.
Arguments:
- queries: bfloat16 [64, 1024, 1024], P('dp', 'ctx'), may hold values from -20 to 20
- keys: bfloat16 [64, 1024, 1024], P('dp', 'ctx'), may hold values from -4 to 4
- values: bfloat16 [64, 1024, 1024], P('dp', 'ctx'), may hold values from -16 to 16
- d_mixed: bfloat16 [64, 1024, 1024], P('dp', 'ctx'), may hold values from -6 to 6
- series_ids: int32 [64, 1024], P('dp', 'ctx'), may hold values from 0 to 15, never falling along the last dimension, each value on 1 to 576 neighbouring positions
- variate_ids: int32 [64, 1024], P('dp', 'ctx'), may hold values from 0 to 3
- variate_bias: float32 [2, 16], replicated, may hold values from -4 to 4
- w_out: bfloat16 [1024, 1024], P('dp'), may hold values from -0.1875 to 0.1875
Outputs:
- mixed: bfloat16 [64, 1024, 1024], P('dp', 'ctx')
- q_grad: bfloat16 [64, 1024, 1024], P('dp', 'ctx')
- k_grad: bfloat16 [64, 1024, 1024], P('dp', 'ctx')
- v_grad: bfloat16 [64, 1024, 1024], P('dp', 'ctx')
- w_grad: float32 [1024, 1024], P('dp')
- bias_grad: float32 [2, 16], replicated
Inputs may be any that keep to these rules, and one draw needn't show every extreme that they name: `series_ids`: within a packed row series numbers never fall; each series spans 1 to 576 consecutive tokens and some series spans exactly 576.
All inputs are finite; a program needn't handle non-finite values.
Results may differ from a plain program's by a relative error of at most 0.015.
Values may be sent and summed in bfloat16 or wider, within the bound.
A program may use at most 128 MiB of HBM per device.

v0:
```python
import functools

import jax
import jax.numpy as jnp
from jax import lax
from jax.sharding import Mesh
from jax.sharding import PartitionSpec as P

HEADS = 16
HEAD_DIM = 64
DP = ("dp_0", "dp_1", "dp_2")
CTX_DP = ("ctx", "dp_0", "dp_1", "dp_2")


NEG = -1e30


def rows_first(arrays, axis, dims):
    turned = [jnp.moveaxis(a, dim, 0) for a, dim in zip(arrays, dims)]
    widths = [t[0].size for t in turned]
    both = jnp.concatenate([t.reshape(-1, w) for t, w in zip(turned, widths)], axis=1)
    result = lax.all_gather(both, axis, axis=0, tiled=True)
    blocks = jnp.split(result, [sum(widths[:k]) for k in range(1, len(widths))], axis=1)
    return tuple(
        (
            jnp.moveaxis(b.reshape(-1, *t.shape[1:]), 0, dim)
            for b, t, dim in zip(blocks, turned, dims)
        )
    )


def sum_in_order(blocks, axes, order):
    inside = blocks.shape[1:]
    blocks = blocks.reshape(*(lax.axis_size(a) for a in axes), *inside)
    blocks = jnp.moveaxis(blocks, order, range(len(axes))).reshape(-1, *inside)
    for k in order:
        blocks = lax.psum_scatter(blocks, axes[k], scatter_dimension=0, tiled=True)
    return blocks[0]


def cut_along(shard, dim, count):
    before, after = (shard.shape[:dim], shard.shape[dim + 1 :])
    return jnp.moveaxis(shard.reshape(*before, count, -1, *after), dim, 0)


def scatter_axes(shard, axes, order, dim):
    count = lax.axis_size(axes)
    return sum_in_order(cut_along(shard, dim, count), axes, order)


def copy_for_each(shard, axis):
    copies = jnp.broadcast_to(shard, (lax.axis_size(axis), *shard.shape))
    return lax.all_to_all(copies, axis, split_axis=0, concat_axis=0, tiled=True)


def taken_together(shard, axis):
    everything = copy_for_each(shard, axis)
    return jnp.sum(everything, axis=0)


def by_axis(shard, axes):
    return functools.reduce(lax.psum, axes, shard)


def by_head(block):
    rows = block.shape[0]
    return block.reshape(rows, block.shape[1] // HEAD_DIM, HEAD_DIM).transpose(1, 0, 2)


def from_heads(block):
    rows = block.shape[1]
    return block.transpose(1, 0, 2).reshape(rows, block.shape[0] * HEAD_DIM)


def on_device(queries, keys, values, d_mixed, series_ids, variate_ids, variate_bias, w_out):
    query = queries[0]
    key_rows = keys[0]
    value_rows = values[0]
    upstream = d_mixed[0]
    tags = series_ids[0] + 1
    variety = variate_ids[0]
    n_ctx = lax.axis_size("ctx")
    scale = HEAD_DIM ** (-0.5)
    w_full = lax.all_gather(w_out, DP, axis=0, tiled=True)
    d_context = lax.dot_general(
        upstream, w_full, (((1,), (1,)), ((), ())), preferred_element_type=jnp.float32
    ).astype(jnp.bfloat16)
    local_heads = HEADS // n_ctx
    spread_q, spread_k, spread_v, spread_d = (
        lax.all_to_all(query, "ctx", split_axis=1, concat_axis=0, tiled=True),
        lax.all_to_all(key_rows, "ctx", split_axis=1, concat_axis=0, tiled=True),
        lax.all_to_all(value_rows, "ctx", split_axis=1, concat_axis=0, tiled=True),
        lax.all_to_all(d_context, "ctx", split_axis=1, concat_axis=0, tiled=True),
    )
    row_tags, row_vars = rows_first((tags, variety), "ctx", (0, 0))
    first_head = lax.axis_index("ctx") * local_heads
    local_bias = lax.dynamic_slice_in_dim(variate_bias, first_head, local_heads, 1).T
    same_all = row_vars[:, None] == row_vars[None, :]
    allowed_all = row_tags[:, None] == row_tags[None, :]

    def per_head(items):
        q_one, k_one, v_one, d_one, bias_one = items
        raw = (
            lax.dot_general(
                q_one, k_one, (((1,), (1,)), ((), ())), preferred_element_type=jnp.float32
            )
            * scale
        )
        scores = jnp.where(allowed_all, raw + jnp.where(same_all, bias_one[0], bias_one[1]), NEG)
        top = jnp.max(scores, axis=1, keepdims=True)
        total = jnp.sum(jnp.where(allowed_all, jnp.exp(scores - top), 0.0), axis=1, keepdims=True)
        lse = top + jnp.log(total)
        probs = jnp.where(allowed_all, jnp.exp(scores - lse), 0.0)
        weights = probs.astype(jnp.bfloat16)
        context_one = jnp.dot(weights, v_one, preferred_element_type=jnp.float32)
        delta_one = jnp.sum(d_one.astype(jnp.float32) * context_one, axis=1)
        dprob = lax.dot_general(
            d_one, v_one, (((1,), (1,)), ((), ())), preferred_element_type=jnp.float32
        )
        dscore = probs * (dprob - delta_one[:, None])
        dround = dscore.astype(jnp.bfloat16)
        q_one_grad = jnp.dot(dround, k_one, preferred_element_type=jnp.float32) * scale
        k_one_grad = (
            lax.dot_general(
                dround, q_one, (((0,), (0,)), ((), ())), preferred_element_type=jnp.float32
            )
            * scale
        )
        v_one_grad = lax.dot_general(
            weights, d_one, (((0,), (0,)), ((), ())), preferred_element_type=jnp.float32
        )
        head_sums = jnp.stack(
            [jnp.sum(jnp.where(same_all, dscore, 0.0)), jnp.sum(jnp.where(same_all, 0.0, dscore))]
        )
        return (
            context_one.astype(jnp.bfloat16),
            q_one_grad.astype(jnp.bfloat16),
            k_one_grad.astype(jnp.bfloat16),
            v_one_grad.astype(jnp.bfloat16),
            head_sums,
        )

    context_h, q_heads, k_heads, v_heads, head_totals = lax.map(
        per_head,
        (by_head(spread_q), by_head(spread_k), by_head(spread_v), by_head(spread_d), local_bias),
    )
    context_bf, q_out, k_out, v_out = (
        lax.all_to_all(from_heads(context_h), "ctx", split_axis=0, concat_axis=1, tiled=True),
        lax.all_to_all(from_heads(q_heads), "ctx", split_axis=0, concat_axis=1, tiled=True),
        lax.all_to_all(from_heads(k_heads), "ctx", split_axis=0, concat_axis=1, tiled=True),
        lax.all_to_all(from_heads(v_heads), "ctx", split_axis=0, concat_axis=1, tiled=True),
    )
    bias_terms = lax.dynamic_update_slice(
        jnp.zeros((2, HEADS), jnp.float32), head_totals.T, (jnp.zeros((), jnp.int32), first_head)
    )
    mixed = jnp.dot(context_bf, w_full, preferred_element_type=jnp.float32).astype(jnp.bfloat16)
    partial_rows = scatter_axes(
        lax.dot_general(
            context_bf, upstream, (((0,), (0,)), ((), ())), preferred_element_type=jnp.float32
        ).astype(jnp.bfloat16),
        DP,
        (2, 0, 1),
        0,
    ).astype(jnp.float32)
    w_grad = taken_together(partial_rows, "ctx")
    bias_grad = by_axis(bias_terms, CTX_DP)
    return (mixed[None], q_out[None], k_out[None], v_out[None], w_grad, bias_grad)


def solution(mesh):
    finer = Mesh(mesh.devices.reshape(mesh.shape["ctx"], 4, 8, 2), ("ctx", "dp_0", "dp_1", "dp_2"))
    placed = (
        P(DP, "ctx", None),
        P(DP, "ctx", None),
        P(DP, "ctx", None),
        P(DP, "ctx", None),
        P(DP, "ctx"),
        P(DP, "ctx"),
        P(),
        P(DP, None),
    )
    return jax.shard_map(
        on_device,
        mesh=finer,
        in_specs=placed,
        out_specs=(
            P(DP, "ctx", None),
            P(DP, "ctx", None),
            P(DP, "ctx", None),
            P(DP, "ctx", None),
            P(DP, None),
            P(),
        ),
        check_vma=False,
    )
```

profile of v0, /device:TPU:1, one launch (start us, length us, event | category | flops | bytes accessed | tf_op | source)
XLA Modules:
  0.0 337.8 jit_solution(8463227029557872238)
XLA Ops:
  9.7 7.6 %all-to-all-start = ((bf16[128,8,128]{0,2,1:T(8,128)(2,1)}), bf16[128,8,128]{0,2,1:T(8,128)(2,1)S(1)}, u32[]{:S(2)}, u32[]{:S(2)}) async-start(bf16[128,8,128]{0,2,1:T(8,128)(2,1)} %bitcast), calls=%async_computation | async-start | bytes 524288 | tf_op jit(solution)/shard_map/all_to_all | solution.py:90
  19.2 7.6 %all-to-all-done = bf16[128,8,128]{0,2,1:T(8,128)(2,1)S(1)} async-done(((bf16[128,8,128]{0,2,1:T(8,128)(2,1)}), bf16[128,8,128]{0,2,1:T(8,128)(2,1)S(1)}, u32[]{:S(2)}, u32[]{:S(2)}) %all-to-all-start) | async-done | bytes 262176 | tf_op jit(solution)/shard_map/all_to_all | solution.py:90
  26.8 3.4 %all-to-all-start.1 = ((bf16[128,8,128]{0,2,1:T(8,128)(2,1)}), bf16[128,8,128]{0,2,1:T(8,128)(2,1)S(1)}, u32[]{:S(2)}, u32[]{:S(2)}) async-start(bf16[128,8,128]{0,2,1:T(8,128)(2,1)} %bitcast.3), calls=%async_computation.1 | async-start | bytes 524288 | tf_op jit(solution)/shard_map/all_to_all | solution.py:91
  32.0 7.6 %all-to-all-done.1 = bf16[128,8,128]{0,2,1:T(8,128)(2,1)S(1)} async-done(((bf16[128,8,128]{0,2,1:T(8,128)(2,1)}), bf16[128,8,128]{0,2,1:T(8,128)(2,1)S(1)}, u32[]{:S(2)}, u32[]{:S(2)}) %all-to-all-start.1) | async-done | bytes 262176 | tf_op jit(solution)/shard_map/all_to_all | solution.py:91
  39.6 3.4 %all-to-all-start.2 = ((bf16[128,8,128]{0,2,1:T(8,128)(2,1)}), bf16[128,8,128]{0,2,1:T(8,128)(2,1)S(1)}, u32[]{:S(2)}, u32[]{:S(2)}) async-start(bf16[128,8,128]{0,2,1:T(8,128)(2,1)} %bitcast.7), calls=%async_computation.2 | async-start | bytes 524288 | tf_op jit(solution)/shard_map/all_to_all | solution.py:92
  44.0 57.0 %all-gather.2.cloned.1.call-done = bf16[1024,1024]{1,0:T(8,128)(2,1)} async-done(((bf16[16,1024]{1,0:T(8,128)(2,1)}), bf16[1024,1024]{1,0:T(8,128)(2,1)}) %all-gather.2.cloned.1.call-update) | async-done | bytes 2097168 | tf_op jit(solution)/shard_map/all_gather | solution.py:84
  104.1 6.5 %all-to-all-start.3 = ((bf16[128,8,128]{2,0,1:T(8,128)(2,1)}), bf16[128,8,128]{2,0,1:T(8,128)(2,1)S(1)}, u32[]{:S(2)}, u32[]{:S(2)}) async-start(bf16[128,8,128]{2,0,1:T(8,128)(2,1)} %bitcast.145), calls=%async_computation.3 | async-start | bytes 524288 | tf_op jit(solution)/shard_map/all_to_all | solution.py:93
  110.7 15.4 %all_gather.6 = s32[1024,2]{0,1:T(2,128)S(1)} all-gather(s32[128,2]{0,1:T(2,128)S(1)} %pad_add_fusion), channel_id=1, replica_groups=mesh['ctx'=8,'dp_0'=4,'dp_1'=8,'dp_2'=2] {'ctx'}, dimensions={0}, use_global_device_ids=true | all-gather | bytes 9216 | tf_op jit(solution)/shard_map/all_gather | solution.py:22
  127.3 28.7 %while.19 = (s32[]{:T(128)}, bf16[2,1024,64]{1,2,0:T(8,128)(2,1)}, bf16[2,1024,64]{1,2,0:T(8,128)(2,1)}, bf16[2,1024,64]{1,2,0:T(8,128)(2,1)}, bf16[2,1024,64]{1...) while((s32[]{:T(128)}, bf16[2,1024,64]{1,2,0:T(8,128)(2,1)}, ...), condition=%wide.region_6.7_spmd.clone, body=%wide.region_0.6_spmd.clone.sunk | while | flops 833157120 | bytes 31676656 | solution.py:143
  134.8 3.0 fusion.83
  149.1 2.9 fusion.83
  157.0 13.7 %all_to_all.136 = bf16[8,128,128]{1,2,0:T(8,128)(2,1)S(1)} all-to-all(bf16[8,128,128]{1,2,0:T(8,128)(2,1)S(1)} %copy.107), channel_id=1, replica_groups=mesh['ctx'=8,'dp_0'=4,'dp_1'=8,'dp_2'=2] {'ctx'}, dimensions={0} | all-to-all | bytes 524288 | tf_op jit(solution)/shard_map/all_to_all | solution.py:148
  173.0 16.8 %reduce-scatter.4.cloned.1.call-done = bf16[32,16,1024]{2,1,0:T(8,128)(2,1)} async-done(((bf16[64,16,1024]{2,1,0:T(8,128)(2,1)}), bf16[32,16,1024]{2,1,0:T(8,128)(2,1)}) %reduce-scatter.4.cloned.1.call-update) | async-done | bytes 1048592 | tf_op jit(solution)/shard_map/reduce_scatter | solution.py:37
  190.7 5.9 %all-to-all-start.5 = ((bf16[8,128,128]{2,1,0:T(8,128)(2,1)}), bf16[8,128,128]{2,1,0:T(8,128)(2,1)S(1)}, u32[]{:S(2)}, u32[]{:S(2)}) async-start(bf16[8,128,128]{2,1,0:T(8,128)(2,1)} %copy.108), calls=%async_computation.5 | async-start | bytes 524288 | tf_op jit(solution)/shard_map/all_to_all | solution.py:149
  197.6 10.2 %all-to-all-done.5 = bf16[8,128,128]{2,1,0:T(8,128)(2,1)S(1)} async-done(((bf16[8,128,128]{2,1,0:T(8,128)(2,1)}), bf16[8,128,128]{2,1,0:T(8,128)(2,1)S(1)}, u32[]{:S(2)}, u32[]{:S(2)}) %all-to-all-start.5) | async-done | bytes 262176 | tf_op jit(solution)/shard_map/all_to_all | solution.py:149
  207.8 3.4 %all-to-all-start.6 = ((bf16[8,128,128]{2,1,0:T(8,128)(2,1)}), bf16[8,128,128]{2,1,0:T(8,128)(2,1)S(1)}, u32[]{:S(2)}, u32[]{:S(2)}) async-start(bf16[8,128,128]{2,1,0:T(8,128)(2,1)} %copy.110), calls=%async_computation.6 | async-start | bytes 524288 | tf_op jit(solution)/shard_map/all_to_all | solution.py:150
  211.3 9.3 %reduce-scatter.6.cloned.1.call-done = bf16[8,16,1024]{2,1,0:T(8,128)(2,1)} async-done(((bf16[32,16,1024]{2,1,0:T(8,128)(2,1)}), bf16[8,16,1024]{2,1,0:T(8,128)(2,1)}) %reduce-scatter.6.cloned.1.call-update) | async-done | bytes 262160 | tf_op jit(solution)/shard_map/reduce_scatter | solution.py:37
  222.5 6.5 %all-to-all-start.7 = ((bf16[8,128,128]{2,1,0:T(8,128)(2,1)}), bf16[8,128,128]{2,1,0:T(8,128)(2,1)S(1)}, u32[]{:S(2)}, u32[]{:S(2)}) async-start(bf16[8,128,128]{2,1,0:T(8,128)(2,1)} %copy.112), calls=%async_computation.7 | async-start | bytes 524288 | tf_op jit(solution)/shard_map/all_to_all | solution.py:151
  229.0 30.8 %reduce-scatter.8.cloned.1.call-done = bf16[1,16,1024]{2,1,0:T(8,128)(2,1)} async-done(((bf16[8,16,1024]{2,1,0:T(8,128)(2,1)}), bf16[1,16,1024]{2,1,0:T(8,128)(2,1)}) %reduce-scatter.8.cloned.1.call-update) | async-done | bytes 32784 | tf_op jit(solution)/shard_map/reduce_scatter | solution.py:37
  261.5 6.5 %all-to-all-start.8 = ((f32[8,16,1024]{2,1,0:T(8,128)}), f32[8,16,1024]{2,1,0:T(8,128)S(1)}, u32[]{:S(2)}, u32[]{:S(2)}) async-start(f32[8,16,1024]{2,1,0:T(8,128)} %broadcast_in_dim.61), calls=%async_computation.11 | async-start | bytes 1048576 | tf_op jit(solution)/shard_map/all_to_all | solution.py:53
  268.1 16.9 %psum.28 = f32[2,16]{1,0:T(2,128)S(1)} all-reduce(f32[2,16]{1,0:T(2,128)S(1)} %dynamic_update_slice.20), channel_id=1, replica_groups=mesh['ctx'=8,'dp_0'=4,'dp_1'=8,'dp_2'=2] {'ctx'}, use_global_device_ids=true, to_apply=%region_11.12 | all-reduce | flops 32 | bytes 256 | tf_op jit(solution)/shard_map/psum | solution.py:62
  285.0 8.9 %psum.29 = f32[2,16]{1,0:T(2,128)S(1)} all-reduce(f32[2,16]{1,0:T(2,128)S(1)} %psum.28), channel_id=1, replica_groups=mesh['ctx'=8,'dp_0'=4,'dp_1'=8,'dp_2'=2] {'dp_0'}, use_global_device_ids=true, to_apply=%region_12.13 | all-reduce | flops 32 | bytes 256 | tf_op jit(solution)/shard_map/psum | solution.py:62
  293.8 13.7 %psum.30 = f32[2,16]{1,0:T(2,128)S(1)} all-reduce(f32[2,16]{1,0:T(2,128)S(1)} %psum.29), channel_id=1, replica_groups=mesh['ctx'=8,'dp_0'=4,'dp_1'=8,'dp_2'=2] {'dp_1'}, use_global_device_ids=true, to_apply=%region_13.14 | all-reduce | flops 32 | bytes 256 | tf_op jit(solution)/shard_map/psum | solution.py:62
  307.6 15.2 %psum.31 = f32[2,16]{1,0:T(2,128)} all-reduce(f32[2,16]{1,0:T(2,128)S(1)} %psum.30), channel_id=1, replica_groups=mesh['ctx'=8,'dp_0'=4,'dp_1'=8,'dp_2'=2] {'dp_2'}, use_global_device_ids=true, to_apply=%region_14.15 | all-reduce | flops 32 | bytes 256 | tf_op jit(solution)/shard_map/psum | solution.py:62
  (101 shorter events, 51.5 us)
Async XLA Ops:
  7.2 93.8 %copy-start = (bf16[1,128,1024]{2,1,0:T(8,128)(2,1)S(1)}, bf16[1,128,1024]{2,1,0:T(8,128)(2,1)}, u32[]{:S(2)}) copy-start(bf16[1,128,1024]{2,1,0:T(8,128)(2,1)} %param.13) | copy-start | bytes 786436
  7.2 103.4 %copy-start.7 = (s32[1,128]{1,0:T(1,128)S(1)}, s32[1,128]{1,0:T(1,128)}, u32[]{:S(2)}) copy-start(s32[1,128]{1,0:T(1,128)} %param.14) | copy-start | bytes 1540
  7.2 103.5 %copy-start.6 = (s32[1,128]{1,0:T(1,128)S(1)}, s32[1,128]{1,0:T(1,128)}, u32[]{:S(2)}) copy-start(s32[1,128]{1,0:T(1,128)} %param.15) | copy-start | bytes 1540
  7.2 93.7 %all-gather.2.cloned.1.call-start = ((), (), s32[]{:S(2)}) async-start(), calls=%async_computation.12 | async-start | bytes 2129920 | tf_op jit(solution)/shard_map/all_gather | solution.py:84
  9.7 17.1 %all-to-all-start = ((bf16[128,8,128]{0,2,1:T(8,128)(2,1)}), bf16[128,8,128]{0,2,1:T(8,128)(2,1)S(1)}, u32[]{:S(2)}, u32[]{:S(2)}) async-start(bf16[128,8,128]{0,2,1:T(8,128)(2,1)} %bitcast), calls=%async_computation | async-start | bytes 524288 | tf_op jit(solution)/shard_map/all_to_all | solution.py:90
  26.8 12.8 %all-to-all-start.1 = ((bf16[128,8,128]{0,2,1:T(8,128)(2,1)}), bf16[128,8,128]{0,2,1:T(8,128)(2,1)S(1)}, u32[]{:S(2)}, u32[]{:S(2)}) async-start(bf16[128,8,128]{0,2,1:T(8,128)(2,1)} %bitcast.3), calls=%async_computation.1 | async-start | bytes 524288 | tf_op jit(solution)/shard_map/all_to_all | solution.py:91
  39.6 64.5 %all-to-all-start.2 = ((bf16[128,8,128]{0,2,1:T(8,128)(2,1)}), bf16[128,8,128]{0,2,1:T(8,128)(2,1)S(1)}, u32[]{:S(2)}, u32[]{:S(2)}) async-start(bf16[128,8,128]{0,2,1:T(8,128)(2,1)} %bitcast.7), calls=%async_computation.2 | async-start | bytes 524288 | tf_op jit(solution)/shard_map/all_to_all | solution.py:92
  104.1 22.9 %all-to-all-start.3 = ((bf16[128,8,128]{2,0,1:T(8,128)(2,1)}), bf16[128,8,128]{2,0,1:T(8,128)(2,1)S(1)}, u32[]{:S(2)}, u32[]{:S(2)}) async-start(bf16[128,8,128]{2,0,1:T(8,128)(2,1)} %bitcast.145), calls=%async_computation.3 | async-start | bytes 524288 | tf_op jit(solution)/shard_map/all_to_all | solution.py:93
  110.6 79.2 %reduce-scatter.4.cloned.1.call-start = ((), (), s32[]{:S(2)}) async-start(), calls=%async_computation.13 | async-start | bytes 3145728 | tf_op jit(solution)/shard_map/reduce_scatter | solution.py:37
  171.4 18.4 %copy-start.5 = (bf16[2,1024,64]{1,2,0:T(8,128)(2,1)S(1)}, bf16[2,1024,64]{1,2,0:T(8,128)(2,1)}, u32[]{:S(2)}) copy-start(bf16[2,1024,64]{1,2,0:T(8,128)(2,1)} %get-tuple-element.78) | copy-start | bytes 786436
  171.4 25.2 %copy-start.4 = (bf16[2,1024,64]{1,2,0:T(8,128)(2,1)S(1)}, bf16[2,1024,64]{1,2,0:T(8,128)(2,1)}, u32[]{:S(2)}) copy-start(bf16[2,1024,64]{1,2,0:T(8,128)(2,1)} %get-tuple-element.79) | copy-start | bytes 786436
  172.9 47.7 %reduce-scatter.6.cloned.1.call-start = ((), (), s32[]{:S(2)}) async-start(), calls=%async_computation.14 | async-start | bytes 1310720 | tf_op jit(solution)/shard_map/reduce_scatter | solution.py:37
  190.7 17.1 %all-to-all-start.5 = ((bf16[8,128,128]{2,1,0:T(8,128)(2,1)}), bf16[8,128,128]{2,1,0:T(8,128)(2,1)S(1)}, u32[]{:S(2)}, u32[]{:S(2)}) async-start(bf16[8,128,128]{2,1,0:T(8,128)(2,1)} %copy.108), calls=%async_computation.5 | async-start | bytes 524288 | tf_op jit(solution)/shard_map/all_to_all | solution.py:149
  196.6 132.8 %copy-start.1 = (bf16[1024,1024]{1,0:T(8,128)(2,1)S(1)}, bf16[1024,1024]{1,0:T(8,128)(2,1)}, u32[]{:S(2)}) copy-start(bf16[1024,1024]{1,0:T(8,128)(2,1)} %all-gather.2.cloned.1.call-done) | copy-start | bytes 6291460
  207.8 14.7 %all-to-all-start.6 = ((bf16[8,128,128]{2,1,0:T(8,128)(2,1)}), bf16[8,128,128]{2,1,0:T(8,128)(2,1)S(1)}, u32[]{:S(2)}, u32[]{:S(2)}) async-start(bf16[8,128,128]{2,1,0:T(8,128)(2,1)} %copy.110), calls=%async_computation.6 | async-start | bytes 524288 | tf_op jit(solution)/shard_map/all_to_all | solution.py:150
  211.2 48.5 %reduce-scatter.8.cloned.1.call-start = ((), (), s32[]{:S(2)}) async-start(), calls=%async_computation.15 | async-start | bytes 294912 | tf_op jit(solution)/shard_map/reduce_scatter | solution.py:37
  222.5 38.9 %copy-start.2 = (bf16[8,128,128]{2,1,0:T(8,128)(2,1)}, bf16[8,128,128]{2,1,0:T(8,128)(2,1)S(1)}, u32[]{:S(2)}) copy-start(bf16[8,128,128]{2,1,0:T(8,128)(2,1)S(1)} %all-to-all-done.6) | copy-start | bytes 786436
  222.5 38.0 %all-to-all-start.7 = ((bf16[8,128,128]{2,1,0:T(8,128)(2,1)}), bf16[8,128,128]{2,1,0:T(8,128)(2,1)S(1)}, u32[]{:S(2)}, u32[]{:S(2)}) async-start(bf16[8,128,128]{2,1,0:T(8,128)(2,1)} %copy.112), calls=%async_computation.7 | async-start | bytes 524288 | tf_op jit(solution)/shard_map/all_to_all | solution.py:151
  260.6 0.9 copy-start.3
  261.5 69.1 %all-to-all-start.8 = ((f32[8,16,1024]{2,1,0:T(8,128)}), f32[8,16,1024]{2,1,0:T(8,128)S(1)}, u32[]{:S(2)}, u32[]{:S(2)}) async-start(f32[8,16,1024]{2,1,0:T(8,128)} %broadcast_in_dim.61), calls=%async_computation.11 | async-start | bytes 1048576 | tf_op jit(solution)/shard_map/all_to_all | solution.py:53
Sparse Core Ops, SparseCore 0:
  11.4 89.5 all-gather.1
  173.1 16.6 reduce-scatter.3
  192.6 27.9 reduce-scatter.5
  223.2 36.5 reduce-scatter.7
where the time goes:
time: 339 us; the launch traced here: 338 us
  waiting for transfers between devices  140 us (41%)
  blocking collectives  83.8 us (25%)
  starting transfers between devices  43.3 us (13%)
  matrix products  25.5 us (8%)
  local copies, waits for them, and re-layouts  23.5 us (7%)
  between operations  14.1 us (4%)
  other arithmetic  7.45 us (2%)
    all_gather x1, waiting for transfers between devices, on_device(): w_full = lax.all_gather(w_out, DP, axis=0, tiled=True)  57 us
    reduce_scatter x3, waiting for transfers between devices, sum_in_order(): blocks = lax.psum_scatter(blocks, axes[k], scatter_dimension=0, tiled=True)  56.9 us
    psum x4, blocking collectives, by_axis(): return functools.reduce(lax.psum, axes, shard)  54.7 us
    all_gather x1, blocking collectives, rows_first(): result = lax.all_gather(both, axis, axis=0, tiled=True)  15.4 us
    all_to_all x1, blocking collectives, on_device(): lax.all_to_all(from_heads(context_h), 'ctx', split_axis=0, concat_axis=1,...  13.7 us
    unnamed x27, local copies, waits for them, and re-layouts  11.1 us
    all_to_all x1, waiting for transfers between devices, on_device(): lax.all_to_all(from_heads(q_heads), 'ctx', split_axis=0, concat_axis=1, t...  10.2 us
    all_to_all x1, waiting for transfers between devices, on_device(): lax.all_to_all(query, 'ctx', split_axis=1, concat_axis=0, tiled=True)  7.65 us
  transfers between devices with their start and end apart: 12, of which 7 were waited for; matrix products, arithmetic and copies ran while one was open for 7% of the time, Pallas kernels for 0%

commit v1 on v0

v1 whole, which is shorter than its diff:
```python
import functools

import jax
import jax.numpy as jnp
from jax import lax
from jax.experimental import pallas as pl
from jax.experimental.pallas import tpu as pltpu
from jax.sharding import Mesh
from jax.sharding import PartitionSpec as P

HEADS = 16
HEAD_DIM = 64
NY, NX, NZ, NC = 8, 4, 8, 2
TOK = 128
ROW = 1024
D = 1024
DP = ("x", "z", "core")
MESH = pl.DeviceIdType.MESH
F32 = jnp.float32
BF16 = jnp.bfloat16
ORDER = (1, 7, 2, 6, 3, 5, 4)
MASK = 2048.0
BQ = 128


def remote(src, dst, ssem, rsem, **where):
    return pltpu.make_async_remote_copy(
        src_ref=src, dst_ref=dst, send_sem=ssem, recv_sem=rsem,
        device_id=where, device_id_type=MESH,
    )


def meet(peers):
    sem = pltpu.get_barrier_semaphore()
    for peer in peers:
        pl.semaphore_signal(sem, inc=1, device_id=peer, device_id_type=MESH)
    pl.semaphore_wait(sem, len(peers))


def others(axis, n):
    me = lax.axis_index(axis)
    return [{axis: lax.rem(me + d, n)} for d in range(1, n)]


def span(i, n=128):
    return pl.ds(pl.multiple_of(i * n, n), n)


def spread(src, dst, ssem, rsem, lsem):
    me = lax.axis_index("ctx")
    copies = []
    for d in ORDER:
        to = lax.rem(me + d, NY)
        c = remote(src.at[:, span(to)], dst.at[span(me), :], ssem.at[d], rsem.at[d], ctx=to)
        c.start()
        copies.append(c)
    c = pltpu.make_async_copy(src.at[:, span(me)], dst.at[span(me), :], lsem)
    c.start()
    copies.append(c)
    return copies


def unspread(src, dst, ssem, rsem, lsem):
    me = lax.axis_index("ctx")
    copies = []
    for d in ORDER:
        to = lax.rem(me + d, NY)
        c = remote(src.at[span(to), :], dst.at[:, span(me)], ssem.at[d], rsem.at[d], ctx=to)
        c.start()
        copies.append(c)
    c = pltpu.make_async_copy(src.at[span(me), :], dst.at[:, span(me)], lsem)
    c.start()
    copies.append(c)
    return copies


def gather_kernel(q, k, v, dm, ser, var, w,
                  qh, kh, vh, dh, ser_o, var_o, wf,
                  dctx, a_s, a_r, a_l, i_s, i_r, i_l, x_s, x_r, z_s, z_r, c_s, c_r, w_l):
    y, x, z, c = (lax.axis_index(a) for a in ("ctx", "x", "z", "core"))
    sib = 1 - c
    up, down = lax.rem(z + 1, NZ), lax.rem(z + NZ - 1, NZ)
    meet(others("ctx", NY) + others("x", NX) + [{"z": up}, {"z": down}, {"core": sib}])
    own = pltpu.make_async_copy(w, wf.at[x, z, c], w_l)
    own.start()
    todo = []
    for d in range(1, NX):
        to = lax.rem(x + d, NX)
        cp = remote(w, wf.at[x, z, c], x_s.at[d], x_r.at[d], x=to)
        cp.start()
        todo.append(cp)
    x_copies = todo[:]
    todo = []
    for n, (src, dst) in enumerate(((ser, ser_o), (var, var_o))):
        for d in ORDER:
            to = lax.rem(y + d, NY)
            cp = remote(src, dst.at[:, span(y)], i_s.at[n, d], i_r.at[n, d], ctx=to)
            cp.start()
            todo.append(cp)
        cp = pltpu.make_async_copy(src, dst.at[:, span(y)], i_l.at[n])
        cp.start()
        todo.append(cp)
    for n, (src, dst) in enumerate(((q, qh), (k, kh), (v, vh))):
        todo += spread(src, dst, a_s.at[n], a_r.at[n], a_l.at[n])

    own.wait()
    arrived = {}
    sub = [lax.rem(x + NX - j, NX) for j in range(NX)]

    def block(zz, j):
        return wf.at[sub[j], zz, c]

    def to_sibling(zz, j, n):
        cp = remote(block(zz, j), block(zz, j), c_s.at[n, j], c_r.at[n, j], core=sib)
        cp.start()
        todo.append(cp)

    for s in range(4):
        zr, zl = lax.rem(z + NZ - s, NZ), lax.rem(z + s, NZ)
        for j in range(NX):
            if s == 0:
                if j > 0:
                    x_copies[j - 1].wait()
            else:
                arrived[(0, s - 1, j)].wait()
            cp = remote(block(zr, j), block(zr, j), z_s.at[0, s, j], z_r.at[0, s, j], z=up)
            cp.start()
            arrived[(0, s, j)] = cp
            if s < 3:
                if s > 0:
                    arrived[(1, s - 1, j)].wait()
                cp = remote(block(zl, j), block(zl, j), z_s.at[1, s, j], z_r.at[1, s, j], z=down)
                cp.start()
                arrived[(1, s, j)] = cp
            to_sibling(zr, j, s)
            if 0 < s < 3:
                to_sibling(zl, j, 4 + s)
    zr, zl = lax.rem(z + NZ - 4, NZ), lax.rem(z + 3, NZ)
    for j in range(NX):
        arrived[(1, 2, j)].wait()
        to_sibling(zl, j, 7)
        arrived[(0, 3, j)].wait()
        to_sibling(zr, j, 4)
    for cp in todo[-8 * NX:]:
        cp.wait()
    todo = todo[:-8 * NX]

    for xi in range(NX):
        rows = wf[xi].reshape(256, D)
        got = lax.dot_general(dm[...], rows, (((1,), (1,)), ((), ())), preferred_element_type=F32)
        dctx[:, 256 * xi:256 * (xi + 1)] = got.astype(BF16)
    todo += spread(dctx, dh, a_s.at[3], a_r.at[3], a_l.at[3])
    for cp in todo:
        cp.wait()


def attention_kernel(qh, kh, vh, dh, ser, var, bias,
                     ctx, dq, dk, dv, bt,
                     base_s, qa_s, ka_s, va_s, qt_s, dkt, dvt):
    me = lax.axis_index("ctx")
    feat = lax.broadcasted_iota(jnp.int32, (128, ROW), 0) % 64
    held = jnp.where(feat < 16, ser[...], var[...])
    want = jnp.where(feat < 16, feat, jnp.where(feat < 28, feat % 4, -1))
    base_t = jnp.where(held == want, 1.0, 0.0)
    base = base_t.T
    base_s[...] = base
    lane = lax.broadcasted_iota(jnp.int32, (1, 128), 1)
    within = lane % 64
    qt_s[...] = (qh[...].astype(F32) * 0.125).T.astype(BF16)
    dkt[...] = jnp.zeros_like(dkt)
    dvt[...] = jnp.zeros_like(dvt)
    for h in range(2):
        mine = (lane // 64) == h
        gap = bias[0, 2 * me + h] - bias[1, 2 * me + h]
        gap = jnp.full((1, 128), gap, F32)
        hi = gap.astype(BF16).astype(F32)
        mid = (gap - hi).astype(BF16).astype(F32)
        low = gap - hi - mid
        coef = jnp.where(within < 16, MASK, jnp.where(within < 20, hi, jnp.where(within < 24, mid, low)))
        qa_s[h] = jnp.where(mine, qh[...].astype(F32) * 0.125, base * coef).astype(BF16)
        ka_s[h] = jnp.where(mine, kh[...].astype(F32), base).astype(BF16)
        va_s[h] = jnp.where(mine, vh[...].astype(F32), 1.0).astype(BF16)

    def step(i, carry):
        rows = span(i, BQ)
        d_blk = dh[rows, :].astype(F32)
        o_blk = base_s[rows, :]
        merged = []
        sums = []
        for h in range(2):
            mine = (lane // 64) == h
            s = lax.dot_general(qa_s[h, rows, :], ka_s[h], (((1,), (1,)), ((), ())),
                                preferred_element_type=F32)
            top = jnp.max(s, axis=1, keepdims=True)
            e = jnp.exp(s - top)
            eb = e.astype(BF16)
            un = jnp.dot(eb, va_s[h], preferred_element_type=F32)
            inv = 1.0 / pltpu.roll(un, 64, 1)
            c = un * inv
            dn = (d_blk * inv).astype(BF16)
            dnf = dn.astype(F32)
            delta = jnp.sum(jnp.where(mine, dnf * c, 0.0), axis=1, keepdims=True)
            hi = delta.astype(BF16).astype(F32)
            mid = (delta - hi).astype(BF16).astype(F32)
            low = delta - hi - mid
            da = jnp.where(within == 0, -hi, jnp.where(within == 1, -mid, jnp.where(within == 2, -low, 0.0)))
            da = jnp.where(mine, dnf, da).astype(BF16)
            t = lax.dot_general(da, va_s[h], (((1,), (1,)), ((), ())), preferred_element_type=F32)
            ds = (e * t).astype(BF16)
            g = jnp.dot(ds, ka_s[h], preferred_element_type=F32)
            half = slice(64 * h, 64 * (h + 1))
            dn_t = jnp.where(mine, dnf, 0.0).T[half].astype(BF16)
            dvt[half, :] += jnp.dot(dn_t, eb, preferred_element_type=F32)
            q_t = qt_s[half, rows]
            dkt[half, :] += jnp.dot(q_t, ds, preferred_element_type=F32)
            wanted = jnp.logical_not(mine) & (within >= 16) & (within < 20)
            u = jnp.where(wanted, g, 0.0)
            sums.append(jnp.sum(u * o_blk, axis=0, keepdims=True))
            sums.append(jnp.sum(u * (1.0 - o_blk), axis=0, keepdims=True))
            merged.append((c, g * 0.125))
        ctx[rows, :] = jnp.where(lane < 64, merged[0][0], merged[1][0]).astype(BF16)
        dq[rows, :] = jnp.where(lane < 64, merged[0][1], merged[1][1]).astype(BF16)
        return tuple(a + b for a, b in zip(carry, sums))

    zero = jnp.zeros((1, 128), F32)
    s0, f0, s1, f1 = lax.fori_loop(0, ROW // BQ, step, (zero,) * 4)
    total = [jnp.sum(a, axis=1, keepdims=True) for a in (s0, f0, s1, f1)]
    row = lax.broadcasted_iota(jnp.int32, (8, 128), 0)
    col = lax.broadcasted_iota(jnp.int32, (8, 128), 1) - 2 * me
    tile = jnp.zeros((8, 128), F32)
    for h in range(2):
        for r in range(2):
            tile = jnp.where((row == r) & (col == h), total[2 * h + r], tile)
    bt[...] = tile
    for b in range(8):
        cols = slice(128 * b, 128 * (b + 1))
        dk[cols, :] = dkt[:, cols].T.astype(BF16)
        dv[cols, :] = dvt[:, cols].T.astype(BF16)


def return_kernel(ctxh, dqh, dkh, dvh, bt, dm, wf,
                  mixed, dq, dk, dv, wg, bg,
                  ctx, g, sa, sb_r, sb_l, rr, rl, acc, xs, xr, ys, yr, bs, br,
                  a_s, a_r, a_l, c_s, c_r, z_s, z_r, x_s, x_r, y_s, y_r, b_s, b_r):
    y, x, z, c = (lax.axis_index(a) for a in ("ctx", "x", "z", "core"))
    sib = 1 - c
    up, down = lax.rem(z + 1, NZ), lax.rem(z + NZ - 1, NZ)
    meet(others("ctx", NY) + others("x", NX) + others("z", NZ) + [{"core": sib}])
    first = unspread(ctxh, ctx, a_s.at[0], a_r.at[0], a_l.at[0])
    todo = []
    for n, (src, dst) in enumerate(((dvh, dv), (dkh, dk), (dqh, dq))):
        todo += unspread(src, dst, a_s.at[n + 1], a_r.at[n + 1], a_l.at[n + 1])
    bsib = remote(bt, br.at[0], b_s.at[0], b_r.at[0], core=sib)
    bsib.start()
    for cp in first:
        cp.wait()
    for xi in range(NX):
        part = ctx[:, 256 * xi:256 * (xi + 1)].astype(F32).T.astype(BF16)
        got = jnp.dot(part, dm[...], preferred_element_type=F32)
        g[xi] = got.astype(BF16).reshape(8, 2, 16, D)

    sibs = {}
    for off in (4, 5, 3, 6, 2, 7, 1, 0):
        zt = lax.rem(z + off, NZ)
        cp = remote(g.at[:, zt, sib], sa.at[:, zt], c_s.at[off], c_r.at[off], core=sib)
        cp.start()
        sibs[off] = cp

    bsib.wait()
    bs[0] = bt[...] + br[0]
    bz = []
    for d in range(1, NZ):
        cp = remote(bs.at[0], br.at[d], b_s.at[d], b_r.at[d], z=lax.rem(z + d, NZ))
        cp.start()
        bz.append(cp)

    def part_sum(off):
        zt = lax.rem(z + off, NZ)
        sibs[off].wait()
        return g[:, zt, c].astype(F32) + sa[:, zt].astype(F32)

    r_cp, l_cp = [], []
    for s in range(4):
        val = part_sum(4 - s)
        if s > 0:
            r_cp[s - 1].wait()
            val = val + rr[s - 1].astype(F32)
        sb_r[s] = val.astype(BF16)
        cp = remote(sb_r.at[s], rr.at[s], z_s.at[0, s], z_r.at[0, s], z=up)
        cp.start()
        r_cp.append(cp)
        if s < 3:
            val = part_sum(5 + s)
            if s > 0:
                l_cp[s - 1].wait()
                val = val + rl[s - 1].astype(F32)
            sb_l[s] = val.astype(BF16)
            cp = remote(sb_l.at[s], rl.at[s], z_s.at[1, s], z_r.at[1, s], z=down)
            cp.start()
            l_cp.append(cp)
        got = jnp.dot(ctx[...], wf[...].reshape(D, D)[:, 256 * s:256 * (s + 1)], preferred_element_type=F32)
        mixed[:, 256 * s:256 * (s + 1)] = got.astype(BF16)
    own = part_sum(0)
    for cp in bz:
        cp.wait()
    tile = bs[0]
    for d in range(1, NZ):
        tile = tile + br[d]
    bs[1] = tile
    bx = []
    for d in range(1, NX):
        cp = remote(bs.at[1], br.at[7 + d], b_s.at[7 + d], b_r.at[7 + d], x=lax.rem(x + d, NX))
        cp.start()
        bx.append(cp)
    l_cp[2].wait()
    r_cp[3].wait()
    own = own + rl[2].astype(F32) + rr[3].astype(F32)
    acc[...] = own
    xs[...] = own.astype(BF16)
    xcp = []
    for d in range(1, NX):
        to = lax.rem(x + d, NX)
        cp = remote(xs.at[to], xr.at[d], x_s.at[d], x_r.at[d], x=to)
        cp.start()
        xcp.append(cp)
    for cp in bx:
        cp.wait()
    bs[2] = bs[1] + br[8] + br[9] + br[10]
    by = []
    for d in range(1, NY):
        cp = remote(bs.at[2], br.at[10 + d], b_s.at[10 + d], b_r.at[10 + d], ctx=lax.rem(y + d, NY))
        cp.start()
        by.append(cp)
    for cp in xcp:
        cp.wait()
    ys[...] = acc[x] + xr[1].astype(F32) + xr[2].astype(F32) + xr[3].astype(F32)
    ycp = []
    for d in ORDER:
        to = lax.rem(y + d, NY)
        cp = remote(ys.at[:, span(to)], yr.at[d], y_s.at[0, d], y_r.at[0, d], ctx=to)
        cp.start()
        ycp.append(cp)
    for cp in by:
        cp.wait()
    tile = bs[2]
    for d in range(1, NY):
        tile = tile + br[10 + d]
    bg[...] = tile
    for cp in ycp:
        cp.wait()
    piece = ys[:, span(y)]
    for d in range(1, NY):
        piece = piece + yr[d]
    yr[0] = piece
    wg[:, span(y)] = piece
    last = []
    for d in ORDER:
        to = lax.rem(y + d, NY)
        cp = remote(yr.at[0], wg.at[:, span(y)], y_s.at[1, d], y_r.at[1, d], ctx=to)
        cp.start()
        last.append(cp)
    for cp in last + todo:
        cp.wait()


VM = pl.BlockSpec(memory_space=pltpu.VMEM)
SM = pl.BlockSpec(memory_space=pltpu.SMEM)
DMA = pltpu.SemaphoreType.DMA
LIMIT = 60 * 1024 * 1024


def sds(shape, dtype):
    return jax.ShapeDtypeStruct(shape, dtype)


def on_device(queries, keys, values, d_mixed, series_ids, variate_ids, variate_bias, w_out):
    heads = sds((ROW, 128), BF16)
    qh, kh, vh, dh, ser, var, wf = pl.pallas_call(
        gather_kernel,
        out_shape=[heads] * 4 + [sds((1, ROW), jnp.int32)] * 2 + [sds((NX, NZ, NC, 16, D), BF16)],
        in_specs=[VM] * 7,
        out_specs=[VM] * 7,
        scratch_shapes=[
            pltpu.VMEM((TOK, D), BF16),
            DMA((4, 8)), DMA((4, 8)), DMA((4,)),
            DMA((2, 8)), DMA((2, 8)), DMA((2,)),
            DMA((4,)), DMA((4,)),
            DMA((2, 4, 4)), DMA((2, 4, 4)),
            DMA((8, 4)), DMA((8, 4)), DMA,
        ],
        compiler_params=pltpu.CompilerParams(collective_id=0, has_side_effects=True, vmem_limit_bytes=LIMIT),
        name="gather",
    )(queries[0], keys[0], values[0], d_mixed[0], series_ids, variate_ids, w_out)
    ctxh, dqh, dkh, dvh, bt = pl.pallas_call(
        attention_kernel,
        out_shape=[heads] * 4 + [sds((8, 128), F32)],
        in_specs=[VM] * 6 + [SM],
        out_specs=[VM] * 5,
        scratch_shapes=[
            pltpu.VMEM((ROW, 128), F32),
            pltpu.VMEM((2, ROW, 128), BF16), pltpu.VMEM((2, ROW, 128), BF16), pltpu.VMEM((2, ROW, 128), BF16),
            pltpu.VMEM((128, ROW), BF16),
            pltpu.VMEM((128, ROW), F32), pltpu.VMEM((128, ROW), F32),
        ],
        compiler_params=pltpu.CompilerParams(vmem_limit_bytes=LIMIT),
        name="attention",
    )(qh, kh, vh, dh, ser, var, variate_bias)
    tokens = sds((TOK, D), BF16)
    mixed, dq, dk, dv, wg, bg = pl.pallas_call(
        return_kernel,
        out_shape=[tokens] * 4 + [sds((16, D), F32), sds((8, 128), F32)],
        in_specs=[VM] * 7,
        out_specs=[VM] * 6,
        scratch_shapes=[
            pltpu.VMEM((TOK, D), BF16),
            pltpu.VMEM((NX, NZ, NC, 16, D), BF16), pltpu.VMEM((NX, NZ, 16, D), BF16),
            pltpu.VMEM((4, NX, 16, D), BF16), pltpu.VMEM((3, NX, 16, D), BF16),
            pltpu.VMEM((4, NX, 16, D), BF16), pltpu.VMEM((3, NX, 16, D), BF16),
            pltpu.VMEM((NX, 16, D), F32), pltpu.VMEM((NX, 16, D), BF16), pltpu.VMEM((NX, 16, D), BF16),
            pltpu.VMEM((16, D), F32), pltpu.VMEM((8, 16, 128), F32),
            pltpu.VMEM((3, 8, 128), F32), pltpu.VMEM((18, 8, 128), F32),
            DMA((4, 8)), DMA((4, 8)), DMA((4,)),
            DMA((8,)), DMA((8,)),
            DMA((2, 4)), DMA((2, 4)),
            DMA((4,)), DMA((4,)),
            DMA((2, 8)), DMA((2, 8)),
            DMA((18,)), DMA((18,)),
        ],
        compiler_params=pltpu.CompilerParams(collective_id=1, has_side_effects=True, vmem_limit_bytes=LIMIT),
        name="giveback",
    )(ctxh, dqh, dkh, dvh, bt, d_mixed[0], wf)
    return mixed[None], dq[None], dk[None], dv[None], wg, bg[:2, :HEADS]


def solution(mesh):
    finer = Mesh(mesh.devices.reshape(NY, NX, NZ, NC), ("ctx", "x", "z", "core"))
    tokens = P(DP, "ctx", None)
    ids = P(DP, "ctx")
    return jax.shard_map(
        on_device,
        mesh=finer,
        in_specs=(tokens, tokens, tokens, tokens, ids, ids, P(), P(DP, None)),
        out_specs=(tokens, tokens, tokens, tokens, P(DP, None), P()),
        check_vma=False,
    )
```

time: 339 us -> 129 us (0.38)
  the two profiles are of different devices: /device:TPU:1 before, /device:TPU:64 now
where the time goes in v1:
time: 129 us
  Pallas kernels  119 us (92%)
  local copies, waits for them, and re-layouts  8.58 us (7%)
    pallas_call x1, Pallas kernels, on_device(): pl.pallas_call(return_kernel, out_shape=[tokens] * 4 + [sds((16, D), F32)...  55.4 us
    pallas_call x1, Pallas kernels, on_device(): pl.pallas_call(gather_kernel, out_shape=[heads] * 4 + [sds((1, ROW), jnp....  45.6 us
    pallas_call x1, Pallas kernels, on_device(): pl.pallas_call(attention_kernel, out_shape=[heads] * 4 + [sds((8, 128), F...  18.4 us
    unnamed x7, local copies, waits for them, and re-layouts  7.31 us

profile of v1, /device:TPU:64, one launch (start us, length us, event | category | flops | bytes accessed | tf_op | source)
XLA Modules:
  0.0 128.6 jit_solution(15991352264692848700)
XLA Ops:
  0.6 45.6 %gather.1 = (bf16[1024,128]{1,0:T(8,128)(2,1)}, bf16[1024,128]{1,0:T(8,128)(2,1)}, bf16[1024,128]{1,0:T(8,128)(2,1)}, bf16[1024,128]{1,0:T(8,128)(2,1)}, s32[1,1...) custom-call(bf16[128,1024]{1,0:T(8,128)(2,1)} %bitcast.10, bf16[128,1024]{1,0:T(8,128)(2,1)} %bitcast.11, ...), custom_call_target="tpu_custom_call" | custom-call | tf_op jit(solution)/shard_map/gather/pallas_call | solution.py:378
  46.2 18.4 %attention.1 = (bf16[1024,128]{1,0:T(8,128)(2,1)}, bf16[1024,128]{1,0:T(8,128)(2,1)}, bf16[1024,128]{1,0:T(8,128)(2,1)}, bf16[1024,128]{1,0:T(8,128)(2,1)}, f32[8,128]{1,0:T(8,128)}) custom-call(bf16[1024,128]{1,0:T(8,128)(2,1)} %get-tuple-element.24.qh, bf16[1024,128]{1,0:T(8,128)(2,1)} %get-tuple-element.25.kh, bf16[1024,128]{1,0:T(8,128)(2,1)} %get-tuple-element.26.vh, ...), custom_call_target="tpu_custom_call" | custom-call | tf_op jit(solution)/shard_map/attention/pallas_call | solution.py:394
  64.6 55.4 %giveback.1 = (bf16[128,1024]{1,0:T(8,128)(2,1)}, bf16[128,1024]{1,0:T(8,128)(2,1)}, bf16[128,1024]{1,0:T(8,128)(2,1)}, bf16[128,1024]{1,0:T(8,128)(2,1)}, f32[16,1024]{1,0:T(8,128)}, /*index=5*/f32[8,128]{1,0:T(8,128)}) custom-call(bf16[1024,128]{1,0:T(8,128)(2,1)} %get-tuple-element.30.ctxh, bf16[1024,128]{1,0:T(8,128)(2,1)} %get-tuple-element.31.dqh, ...), custom_call_target="tpu_custom_call" | custom-call | tf_op jit(solution)/shard_map/giveback/pallas_call | solution.py:409
  120.0 0.0 copy-start
  120.0 1.3 slice.3
  121.3 1.7 %copy.19 = bf16[1,128,1024]{2,1,0:T(8,128)(2,1)} copy(bf16[1,128,1024]{2,1,0:T(8,128)(2,1)} %bitcast.16) | data formatting | bytes 524288
  123.0 1.7 %copy.20 = bf16[1,128,1024]{2,1,0:T(8,128)(2,1)} copy(bf16[1,128,1024]{2,1,0:T(8,128)(2,1)} %bitcast.15) | data formatting | bytes 524288
  124.6 1.7 %copy.21 = bf16[1,128,1024]{2,1,0:T(8,128)(2,1)} copy(bf16[1,128,1024]{2,1,0:T(8,128)(2,1)} %bitcast.14) | data formatting | bytes 524288
  126.3 1.7 %copy.22 = bf16[1,128,1024]{2,1,0:T(8,128)(2,1)} copy(bf16[1,128,1024]{2,1,0:T(8,128)(2,1)} %bitcast.13) | data formatting | bytes 524288
  128.0 0.0 copy-done
  128.0 0.6 copy.23
Async XLA Ops:
  120.0 8.0 %copy-start = (f32[16,1024]{1,0:T(8,128)S(1)}, f32[16,1024]{1,0:T(8,128)}, u32[]{:S(2)}) copy-start(f32[16,1024]{1,0:T(8,128)} %get-tuple-element.52) | copy-start | bytes 196612

commit v2 on v1

v2 whole, which is shorter than its diff:
```python
import functools

import jax
import jax.numpy as jnp
from jax import lax
from jax.experimental import pallas as pl
from jax.experimental.pallas import tpu as pltpu
from jax.sharding import Mesh
from jax.sharding import PartitionSpec as P

HEADS = 16
HEAD_DIM = 64
NY, NX, NZ, NC = 8, 4, 8, 2
TOK = 128
ROW = 1024
D = 1024
DP = ("x", "z", "core")
MESH = pl.DeviceIdType.MESH
F32 = jnp.float32
BF16 = jnp.bfloat16
ORDER = (1, 7, 2, 6, 3, 5, 4)
MASK = 2048.0
BQ = 256


def remote(src, dst, ssem, rsem, **where):
    return pltpu.make_async_remote_copy(
        src_ref=src, dst_ref=dst, send_sem=ssem, recv_sem=rsem,
        device_id=where, device_id_type=MESH,
    )


def meet(peers):
    sem = pltpu.get_barrier_semaphore()
    for peer in peers:
        pl.semaphore_signal(sem, inc=1, device_id=peer, device_id_type=MESH)
    pl.semaphore_wait(sem, len(peers))


def others(axis, n):
    me = lax.axis_index(axis)
    return [{axis: lax.rem(me + d, n)} for d in range(1, n)]


def span(i, n=128):
    return pl.ds(pl.multiple_of(i * n, n), n)


def spread(src, dst, ssem, rsem, lsem):
    me = lax.axis_index("ctx")
    copies = []
    for d in ORDER:
        to = lax.rem(me + d, NY)
        c = remote(src.at[:, span(to)], dst.at[span(me), :], ssem.at[d], rsem.at[d], ctx=to)
        c.start()
        copies.append(c)
    c = pltpu.make_async_copy(src.at[:, span(me)], dst.at[span(me), :], lsem)
    c.start()
    copies.append(c)
    return copies


def unspread(src, dst, ssem, rsem, lsem):
    me = lax.axis_index("ctx")
    copies = []
    for d in ORDER:
        to = lax.rem(me + d, NY)
        c = remote(src.at[span(to), :], dst.at[:, span(me)], ssem.at[d], rsem.at[d], ctx=to)
        c.start()
        copies.append(c)
    c = pltpu.make_async_copy(src.at[span(me), :], dst.at[:, span(me)], lsem)
    c.start()
    copies.append(c)
    return copies


def fused_kernel(q, k, v, dm, ser, var, w, bias,
                 mixed, dq, dk, dv, wg, bg,
                 qh, kh, vh, dh, ser_o, var_o, wf, dctx,
                 base_s, qa_s, ka_s, va_s, qt_s, eb_s, ds_s, c_s32, inv_s, dn_s, dnt_s, dkt, dvt,
                 ctxh, dqh, dkh, dvh,
                 ctx, g, sa, sb_r, sb_l, rr, rl, acc, xs, xr, ys, yr, bs, br,
                 a_s, a_r, a_l, i_s, i_r, i_l, wx_s, wx_r, wz_s, wz_r, wc_s, wc_r, w_l,
                 c_s, c_r, z_s, z_r, x_s, x_r, y_s, y_r, b_s, b_r):
    y, x, z, c = (lax.axis_index(a) for a in ("ctx", "x", "z", "core"))
    sib = 1 - c
    up, down = lax.rem(z + 1, NZ), lax.rem(z + NZ - 1, NZ)
    meet(others("ctx", NY) + others("x", NX) + others("z", NZ) + [{"core": sib}])

    own = pltpu.make_async_copy(w, wf.at[x, z, c], w_l)
    own.start()
    x_copies = []
    for d in range(1, NX):
        cp = remote(w, wf.at[x, z, c], wx_s.at[d], wx_r.at[d], x=lax.rem(x + d, NX))
        cp.start()
        x_copies.append(cp)
    ids = []
    for n, (src, dst) in enumerate(((ser, ser_o), (var, var_o))):
        for d in ORDER:
            cp = remote(src, dst.at[:, span(y)], i_s.at[n, d], i_r.at[n, d], ctx=lax.rem(y + d, NY))
            cp.start()
            ids.append(cp)
        cp = pltpu.make_async_copy(src, dst.at[:, span(y)], i_l.at[n])
        cp.start()
        ids.append(cp)
    ins = []
    for n, (src, dst) in enumerate(((q, qh), (k, kh), (v, vh))):
        ins.append(spread(src, dst, a_s.at[n], a_r.at[n], a_l.at[n]))

    own.wait()
    arrived = {}
    siblings = []
    sub = [lax.rem(x + NX - j, NX) for j in range(NX)]

    def block(zz, j):
        return wf.at[sub[j], zz, c]

    def to_sibling(zz, j, n):
        cp = remote(block(zz, j), block(zz, j), wc_s.at[n, j], wc_r.at[n, j], core=sib)
        cp.start()
        siblings.append(cp)

    for s in range(4):
        zr, zl = lax.rem(z + NZ - s, NZ), lax.rem(z + s, NZ)
        for j in range(NX):
            if s == 0:
                if j > 0:
                    x_copies[j - 1].wait()
            else:
                arrived[(0, s - 1, j)].wait()
            cp = remote(block(zr, j), block(zr, j), wz_s.at[0, s, j], wz_r.at[0, s, j], z=up)
            cp.start()
            arrived[(0, s, j)] = cp
            if s < 3:
                if s > 0:
                    arrived[(1, s - 1, j)].wait()
                cp = remote(block(zl, j), block(zl, j), wz_s.at[1, s, j], wz_r.at[1, s, j], z=down)
                cp.start()
                arrived[(1, s, j)] = cp
            to_sibling(zr, j, s)
            if 0 < s < 3:
                to_sibling(zl, j, 4 + s)
    zr, zl = lax.rem(z + NZ - 4, NZ), lax.rem(z + 3, NZ)
    for j in range(NX):
        arrived[(1, 2, j)].wait()
        to_sibling(zl, j, 7)
        arrived[(0, 3, j)].wait()
        to_sibling(zr, j, 4)
    for cp in siblings:
        cp.wait()
    for xi in range(NX):
        rows = wf[xi].reshape(256, D)
        got = lax.dot_general(dm[...], rows, (((1,), (1,)), ((), ())), preferred_element_type=F32)
        dctx[:, 256 * xi:256 * (xi + 1)] = got.astype(BF16)
    ins.append(spread(dctx, dh, a_s.at[3], a_r.at[3], a_l.at[3]))

    for cp in ids + ins[0] + ins[1]:
        cp.wait()
    feat = lax.broadcasted_iota(jnp.int32, (128, ROW), 0) % 64
    held = jnp.where(feat < 16, ser_o[...], var_o[...])
    want = jnp.where(feat < 16, feat, jnp.where(feat < 28, feat % 4, -1))
    base = jnp.where(held == want, 1.0, 0.0).T
    base_s[...] = base
    lane = lax.broadcasted_iota(jnp.int32, (1, 128), 1)
    within = lane % 64
    half = [slice(0, 64), slice(64, 128)]
    mine = [lane < 64, lane >= 64]
    qt_s[...] = (qh[...].astype(F32) * 0.125).T.astype(BF16)
    for h in range(2):
        gap = jnp.full((1, 128), bias[0, 2 * y + h] - bias[1, 2 * y + h], F32)
        hi = gap.astype(BF16).astype(F32)
        mid = (gap - hi).astype(BF16).astype(F32)
        low = gap - hi - mid
        coef = jnp.where(within < 16, MASK, jnp.where(within < 20, hi, jnp.where(within < 24, mid, low)))
        qa_s[h] = jnp.where(mine[h], qh[...].astype(F32) * 0.125, base * coef).astype(BF16)
        ka_s[h] = jnp.where(mine[h], kh[...].astype(F32), base).astype(BF16)
    for cp in ins[2]:
        cp.wait()
    for h in range(2):
        va_s[h] = jnp.where(mine[h], vh[...].astype(F32), 1.0).astype(BF16)

    def forward(i, carry):
        rows = span(i, BQ)
        un = []
        for h in range(2):
            s = lax.dot_general(qa_s[h, rows, :], ka_s[h], (((1,), (1,)), ((), ())),
                                preferred_element_type=F32)
            top = jnp.max(s, axis=1, keepdims=True)
            e = jnp.exp(s - top).astype(BF16)
            eb_s[h, rows, :] = e
            un.append(jnp.dot(e, va_s[h], preferred_element_type=F32))
        inv = 1.0 / pltpu.roll(jnp.where(mine[0], un[1], un[0]), 64, 1)
        mix = jnp.where(mine[0], un[0], un[1]) * inv
        inv_s[rows, :] = inv
        c_s32[rows, :] = mix
        ctxh[rows, :] = mix.astype(BF16)
        return carry

    lax.fori_loop(0, ROW // BQ, forward, 0)
    back = [unspread(ctxh, ctx, a_s.at[4], a_r.at[4], a_l.at[4])]

    for cp in ins[3]:
        cp.wait()
    dn_s[...] = (dh[...].astype(F32) * inv_s[...]).astype(BF16)
    dnt_s[...] = dn_s[...].astype(F32).T.astype(BF16)

    def values_grad(j, carry):
        cols = span(j, 256)
        for h in range(2):
            dvt[half[h], :] = jnp.dot(dnt_s[half[h], :], eb_s[h, :, cols], preferred_element_type=F32)
        dvh[cols, :] = dvt[...].T.astype(BF16)
        return carry

    lax.fori_loop(0, ROW // 256, values_grad, 0)
    back.append(unspread(dvh, dv, a_s.at[5], a_r.at[5], a_l.at[5]))

    def queries_grad(i, carry):
        rows = span(i, BQ)
        dnf = dn_s[rows, :].astype(F32)
        prod = dnf * c_s32[rows, :]
        o_blk = base_s[rows, :]
        outs, sums = [], []
        for h in range(2):
            delta = jnp.sum(jnp.where(mine[h], prod, 0.0), axis=1, keepdims=True)
            hi = delta.astype(BF16).astype(F32)
            mid = (delta - hi).astype(BF16).astype(F32)
            low = delta - hi - mid
            da = jnp.where(within == 0, -hi, jnp.where(within == 1, -mid, jnp.where(within == 2, -low, 0.0)))
            da = jnp.where(mine[h], dnf, da).astype(BF16)
            t = lax.dot_general(da, va_s[h], (((1,), (1,)), ((), ())), preferred_element_type=F32)
            ds = (eb_s[h, rows, :].astype(F32) * t).astype(BF16)
            ds_s[h, rows, :] = ds
            got = jnp.dot(ds, ka_s[h], preferred_element_type=F32)
            u = jnp.where(mine[1 - h] & (within >= 16) & (within < 20), got, 0.0)
            sums.append(jnp.sum(u * o_blk, axis=0, keepdims=True))
            sums.append(jnp.sum(u * (1.0 - o_blk), axis=0, keepdims=True))
            outs.append(got)
        dqh[rows, :] = (jnp.where(mine[0], outs[0], outs[1]) * 0.125).astype(BF16)
        return tuple(a + b for a, b in zip(carry, sums))

    zero = jnp.zeros((1, 128), F32)
    sums = lax.fori_loop(0, ROW // BQ, queries_grad, (zero,) * 4)
    back.append(unspread(dqh, dq, a_s.at[6], a_r.at[6], a_l.at[6]))
    total = [jnp.sum(a, axis=1, keepdims=True) for a in sums]
    row = lax.broadcasted_iota(jnp.int32, (8, 128), 0)
    col = lax.broadcasted_iota(jnp.int32, (8, 128), 1) - 2 * y
    tile = jnp.zeros((8, 128), F32)
    for h in range(2):
        for r in range(2):
            tile = jnp.where((row == r) & (col == h), total[2 * h + r], tile)
    bs[3] = tile
    bsib = remote(bs.at[3], br.at[0], b_s.at[0], b_r.at[0], core=sib)
    bsib.start()

    for cp in back[0]:
        cp.wait()
    for xi in range(NX):
        part = ctx[:, 256 * xi:256 * (xi + 1)].astype(F32).T.astype(BF16)
        got = jnp.dot(part, dm[...], preferred_element_type=F32)
        g[xi] = got.astype(BF16).reshape(8, 2, 16, D)
    sibs = {}
    for off in (4, 5, 3, 6, 2, 7, 1, 0):
        zt = lax.rem(z + off, NZ)
        cp = remote(g.at[:, zt, sib], sa.at[:, zt], c_s.at[off], c_r.at[off], core=sib)
        cp.start()
        sibs[off] = cp

    def keys_grad(j, carry):
        cols = span(j, 256)
        for h in range(2):
            dkt[half[h], :] = jnp.dot(qt_s[half[h], :], ds_s[h, :, cols], preferred_element_type=F32)
        dkh[cols, :] = dkt[...].T.astype(BF16)
        return carry

    lax.fori_loop(0, ROW // 256, keys_grad, 0)
    back.append(unspread(dkh, dk, a_s.at[7], a_r.at[7], a_l.at[7]))

    bsib.wait()
    bs[0] = bs[3] + br[0]
    bz = []
    for d in range(1, NZ):
        cp = remote(bs.at[0], br.at[d], b_s.at[d], b_r.at[d], z=lax.rem(z + d, NZ))
        cp.start()
        bz.append(cp)

    def part_sum(off):
        zt = lax.rem(z + off, NZ)
        sibs[off].wait()
        return g[:, zt, c].astype(F32) + sa[:, zt].astype(F32)

    r_cp, l_cp = [], []
    for s in range(4):
        val = part_sum(4 - s)
        if s > 0:
            r_cp[s - 1].wait()
            val = val + rr[s - 1].astype(F32)
        sb_r[s] = val.astype(BF16)
        cp = remote(sb_r.at[s], rr.at[s], z_s.at[0, s], z_r.at[0, s], z=up)
        cp.start()
        r_cp.append(cp)
        if s < 3:
            val = part_sum(5 + s)
            if s > 0:
                l_cp[s - 1].wait()
                val = val + rl[s - 1].astype(F32)
            sb_l[s] = val.astype(BF16)
            cp = remote(sb_l.at[s], rl.at[s], z_s.at[1, s], z_r.at[1, s], z=down)
            cp.start()
            l_cp.append(cp)
        got = jnp.dot(ctx[...], wf[...].reshape(D, D)[:, 256 * s:256 * (s + 1)], preferred_element_type=F32)
        mixed[:, 256 * s:256 * (s + 1)] = got.astype(BF16)
    own = part_sum(0)
    for cp in bz:
        cp.wait()
    tile = bs[0]
    for d in range(1, NZ):
        tile = tile + br[d]
    bs[1] = tile
    bx = []
    for d in range(1, NX):
        cp = remote(bs.at[1], br.at[7 + d], b_s.at[7 + d], b_r.at[7 + d], x=lax.rem(x + d, NX))
        cp.start()
        bx.append(cp)
    l_cp[2].wait()
    r_cp[3].wait()
    own = own + rl[2].astype(F32) + rr[3].astype(F32)
    acc[...] = own
    xs[...] = own.astype(BF16)
    xcp = []
    for d in range(1, NX):
        to = lax.rem(x + d, NX)
        cp = remote(xs.at[to], xr.at[d], x_s.at[d], x_r.at[d], x=to)
        cp.start()
        xcp.append(cp)
    for cp in bx:
        cp.wait()
    bs[2] = bs[1] + br[8] + br[9] + br[10]
    by = []
    for d in range(1, NY):
        cp = remote(bs.at[2], br.at[10 + d], b_s.at[10 + d], b_r.at[10 + d], ctx=lax.rem(y + d, NY))
        cp.start()
        by.append(cp)
    for cp in xcp:
        cp.wait()
    ys[...] = acc[x] + xr[1].astype(F32) + xr[2].astype(F32) + xr[3].astype(F32)
    ycp = []
    for d in ORDER:
        to = lax.rem(y + d, NY)
        cp = remote(ys.at[:, span(to)], yr.at[d], y_s.at[0, d], y_r.at[0, d], ctx=to)
        cp.start()
        ycp.append(cp)
    for cp in by:
        cp.wait()
    tile = bs[2]
    for d in range(1, NY):
        tile = tile + br[10 + d]
    bg[...] = tile
    for cp in ycp:
        cp.wait()
    piece = ys[:, span(y)]
    for d in range(1, NY):
        piece = piece + yr[d]
    yr[0] = piece
    wg[:, span(y)] = piece
    last = []
    for d in ORDER:
        to = lax.rem(y + d, NY)
        cp = remote(yr.at[0], wg.at[:, span(y)], y_s.at[1, d], y_r.at[1, d], ctx=to)
        cp.start()
        last.append(cp)
    for cp in last + back[1] + back[2] + back[3]:
        cp.wait()


def finish_kernel(*refs):
    for src, dst in zip(refs[:6], refs[6:]):
        dst[...] = src[:dst.shape[0], :dst.shape[1]]


VM = pl.BlockSpec(memory_space=pltpu.VMEM)
SM = pl.BlockSpec(memory_space=pltpu.SMEM)
ANY = pl.BlockSpec(memory_space=pl.ANY)
DMA = pltpu.SemaphoreType.DMA
LIMIT = 62 * 1024 * 1024


def sds(shape, dtype):
    return jax.ShapeDtypeStruct(shape, dtype)


def on_device(queries, keys, values, d_mixed, series_ids, variate_ids, variate_bias, w_out):
    tokens = sds((TOK, D), BF16)
    wide = pltpu.VMEM((ROW, 128), BF16)
    wide32 = pltpu.VMEM((ROW, 128), F32)
    pair = pltpu.VMEM((2, ROW, 128), BF16)
    square = pltpu.VMEM((2, ROW, ROW), BF16)
    results = pl.pallas_call(
        fused_kernel,
        out_shape=[tokens] * 4 + [sds((16, D), F32), sds((8, 128), F32)],
        in_specs=[ANY] * 3 + [VM] * 4 + [SM],
        out_specs=[VM] * 6,
        scratch_shapes=[
            wide, wide, wide, wide,
            pltpu.VMEM((1, ROW), jnp.int32), pltpu.VMEM((1, ROW), jnp.int32),
            pltpu.VMEM((NX, NZ, NC, 16, D), BF16), pltpu.VMEM((TOK, D), BF16),
            wide32, pair, pair, pair, pltpu.VMEM((128, ROW), BF16),
            square, square, wide32, wide32, wide, pltpu.VMEM((128, ROW), BF16),
            pltpu.VMEM((128, 256), F32), pltpu.VMEM((128, 256), F32),
            wide, wide, wide, wide,
            pltpu.VMEM((TOK, D), BF16),
            pltpu.VMEM((NX, NZ, NC, 16, D), BF16), pltpu.VMEM((NX, NZ, 16, D), BF16),
            pltpu.VMEM((4, NX, 16, D), BF16), pltpu.VMEM((3, NX, 16, D), BF16),
            pltpu.VMEM((4, NX, 16, D), BF16), pltpu.VMEM((3, NX, 16, D), BF16),
            pltpu.VMEM((NX, 16, D), F32), pltpu.VMEM((NX, 16, D), BF16), pltpu.VMEM((NX, 16, D), BF16),
            pltpu.VMEM((16, D), F32), pltpu.VMEM((8, 16, 128), F32),
            pltpu.VMEM((4, 8, 128), F32), pltpu.VMEM((18, 8, 128), F32),
            DMA((8, 8)), DMA((8, 8)), DMA((8,)),
            DMA((2, 8)), DMA((2, 8)), DMA((2,)),
            DMA((4,)), DMA((4,)),
            DMA((2, 4, 4)), DMA((2, 4, 4)),
            DMA((8, 4)), DMA((8, 4)), DMA,
            DMA((8,)), DMA((8,)),
            DMA((2, 4)), DMA((2, 4)),
            DMA((4,)), DMA((4,)),
            DMA((2, 8)), DMA((2, 8)),
            DMA((18,)), DMA((18,)),
        ],
        compiler_params=pltpu.CompilerParams(collective_id=0, has_side_effects=True, vmem_limit_bytes=LIMIT),
        name="fused",
    )(queries[0], keys[0], values[0], d_mixed[0], series_ids, variate_ids, w_out, variate_bias)
    mixed, dq, dk, dv, wg, bg = pl.pallas_call(
        finish_kernel,
        out_shape=[tokens] * 4 + [sds((16, D), F32), sds((2, HEADS), F32)],
        in_specs=[VM] * 6,
        out_specs=[VM] * 6,
        compiler_params=pltpu.CompilerParams(vmem_limit_bytes=LIMIT),
        name="finish",
    )(*results)
    return mixed[None], dq[None], dk[None], dv[None], wg, bg


def solution(mesh):
    finer = Mesh(mesh.devices.reshape(NY, NX, NZ, NC), ("ctx", "x", "z", "core"))
    tokens = P(DP, "ctx", None)
    ids = P(DP, "ctx")
    return jax.shard_map(
        on_device,
        mesh=finer,
        in_specs=(tokens, tokens, tokens, tokens, ids, ids, P(), P(DP, None)),
        out_specs=(tokens, tokens, tokens, tokens, P(DP, None), P()),
        check_vma=False,
    )
```

time: 129 us -> 93.2 us (0.72)
  the two profiles are of different devices: /device:TPU:64 before, /device:TPU:8 now
where the time goes in v2:
time: 93.2 us; the launch traced here: 93.1 us
  Pallas kernels  92.4 us (99%)
    pallas_call x1, Pallas kernels, on_device(): pl.pallas_call(fused_kernel, out_shape=[tokens] * 4 + [sds((16, D), F32),...  90.3 us
    pallas_call x1, Pallas kernels, on_device(): pl.pallas_call(finish_kernel, out_shape=[tokens] * 4 + [sds((16, D), F32)...  2.19 us

profile of v2, /device:TPU:8, one launch (start us, length us, event | category | flops | bytes accessed | tf_op | source)
XLA Modules:
  0.0 93.1 jit_solution(3491985905206427227)
XLA Ops:
  0.6 90.3 %fused.1 = (bf16[128,1024]{1,0:T(8,128)(2,1)}, bf16[128,1024]{1,0:T(8,128)(2,1)}, bf16[128,1024]{1,0:T(8,128)(2,1)}, bf16[128,1024]{1,0:T(8,128)(2,1)}, f32[16,1024]{1,0:T(8,128)}, /*index=5*/f32[8,128]{1,0:T(8,128)}) custom-call(bf16[128,1024]{1,0:T(8,128)(2,1)} %bitcast.8, bf16[128,1024]{1,0:T(8,128)(2,1)} %bitcast.9, bf16[128,1024]{1,0:T(8,128)(2,1)} %bitcast.10, ...), custom_call_target="tpu_custom_call" | custom-call | tf_op jit(solution)/shard_map/fused/pallas_call | solution.py:397
  90.9 2.2 %finish.1 = (bf16[128,1024]{1,0:T(8,128)(2,1)}, bf16[128,1024]{1,0:T(8,128)(2,1)}, bf16[128,1024]{1,0:T(8,128)(2,1)}, bf16[128,1024]{1,0:T(8,128)(2,1)}, f32[16,1024]{1,0:T(8,128)}, /*index=5*/f32[2,16]{1,0:T(2,128)}) custom-call(bf16[128,1024]{1,0:T(8,128)(2,1)} %get-tuple-element.18.refs_0_, bf16[128,1024]{1,0:T(8,128)(2,1)} %get-tuple-element.19.refs_1_, ...), custom_call_target="tpu_custom_call" | custom-call | tf_op jit(solution)/shard_map/finish/pallas_call | solution.py:431

commit v3 on v2

v3 whole, which is shorter than its diff:
```python
import functools

import jax
import jax.numpy as jnp
from jax import lax
from jax.experimental import pallas as pl
from jax.experimental.pallas import tpu as pltpu
from jax.sharding import Mesh
from jax.sharding import PartitionSpec as P

HEADS = 16
HEAD_DIM = 64
NY, NX, NZ, NC = 8, 4, 8, 2
TOK = 128
ROW = 1024
D = 1024
DP = ("x", "z", "core")
MESH = pl.DeviceIdType.MESH
F32 = jnp.float32
BF16 = jnp.bfloat16
ORDER = (1, 7, 2, 6, 3, 5, 4)
LATE = (4, 5, 3, 6, 2, 7, 1, 0)
MASK = 2048.0
BQ = 256


def remote(src, dst, ssem, rsem, **where):
    return pltpu.make_async_remote_copy(
        src_ref=src, dst_ref=dst, send_sem=ssem, recv_sem=rsem,
        device_id=where, device_id_type=MESH,
    )


def meet(peers):
    sem = pltpu.get_barrier_semaphore()
    for peer in peers:
        pl.semaphore_signal(sem, inc=1, device_id=peer, device_id_type=MESH)
    pl.semaphore_wait(sem, len(peers))


def others(axis, n):
    me = lax.axis_index(axis)
    return [{axis: lax.rem(me + d, n)} for d in range(1, n)]


def span(i, n=128):
    return pl.ds(pl.multiple_of(i * n, n), n)


def spread(src, dst, ssem, rsem, lsem):
    me = lax.axis_index("ctx")
    copies = []
    for d in ORDER:
        to = lax.rem(me + d, NY)
        c = remote(src.at[:, span(to)], dst.at[span(me), :], ssem.at[d], rsem.at[d], ctx=to)
        c.start()
        copies.append(c)
    c = pltpu.make_async_copy(src.at[:, span(me)], dst.at[span(me), :], lsem)
    c.start()
    copies.append(c)
    return copies


def unspread(src, dst, ssem, rsem, lsem):
    me = lax.axis_index("ctx")
    copies = []
    for d in ORDER:
        to = lax.rem(me + d, NY)
        c = remote(src.at[span(to), :], dst.at[:, span(me)], ssem.at[d], rsem.at[d], ctx=to)
        c.start()
        copies.append(c)
    c = pltpu.make_async_copy(src.at[span(me), :], dst.at[:, span(me)], lsem)
    c.start()
    copies.append(c)
    return copies


def fused_kernel(q, k, v, dm_in, ser, var, w, bias,
                 mixed_o, dq, dk, dv, wg, bg,
                 dm, mixed, qh, kh, vh, dh, ser_o, var_o, wf, dctx,
                 base_s, qa_s, ka_s, va_s, qt_s, eb_s, ds_s, c_s32, inv_s, dn_s, dnt_s, dkt, dvt,
                 ctxh, dqh, dkh, dvh,
                 ctx, g, sa, hs, hf, hr, zs, zr, ys, yr, bs, br,
                 a_s, a_r, a_l, i_s, i_r, i_l, wz_s, wz_r, wx_s, wx_r, wc_s, wc_r, w_l,
                 c_s, c_r, x_s, x_r, z_s, z_r, y_s, y_r, b_s, b_r):
    y, x, z, c = (lax.axis_index(a) for a in ("ctx", "x", "z", "core"))
    sib = 1 - c
    dm_copy = pltpu.make_async_copy(dm_in, dm, w_l.at[1])
    dm_copy.start()
    own = pltpu.make_async_copy(w, wf.at[x, z, c], w_l.at[0])
    own.start()
    meet(others("ctx", NY) + others("x", NX) + others("z", NZ) + [{"core": sib}])

    from_z, from_x = {}, {}
    for d in ORDER:
        cp = remote(w, wf.at[x, z, c], wz_s.at[d], wz_r.at[d], z=lax.rem(z + d, NZ))
        cp.start()
        from_z[d] = cp

    def to_x(e):
        src = wf.at[x, lax.rem(z + NZ - e, NZ), c]
        for d in range(1, NX):
            cp = remote(w if e == 0 else src, src, wx_s.at[e, d], wx_r.at[e, d], x=lax.rem(x + d, NX))
            cp.start()
            from_x[e, d] = cp

    to_x(0)
    ids = []
    for n, (src, dst) in enumerate(((ser, ser_o), (var, var_o))):
        for d in ORDER:
            cp = remote(src, dst.at[:, span(y)], i_s.at[n, d], i_r.at[n, d], ctx=lax.rem(y + d, NY))
            cp.start()
            ids.append(cp)
        cp = pltpu.make_async_copy(src, dst.at[:, span(y)], i_l.at[n])
        cp.start()
        ids.append(cp)
    ins = []
    for n, (src, dst) in enumerate(((q, qh), (k, kh), (v, vh))):
        ins.append(spread(src, dst, a_s.at[n], a_r.at[n], a_l.at[n]))

    own.wait()
    siblings = []

    def to_sibling(e):
        for d in range(1, NX):
            from_x[e, d].wait()
        part = wf.at[:, lax.rem(z + NZ - e, NZ), c]
        cp = remote(part, part, wc_s.at[e], wc_r.at[e], core=sib)
        cp.start()
        siblings.append(cp)

    for e in ORDER:
        from_z[e].wait()
        to_x(e)

    for cp in ids + ins[0] + ins[1]:
        cp.wait()
    feat = lax.broadcasted_iota(jnp.int32, (128, ROW), 0) % 64
    held = jnp.where(feat < 16, ser_o[...], var_o[...])
    want = jnp.where(feat < 16, feat, jnp.where(feat < 28, feat % 4, -1))
    base = jnp.where(held == want, 1.0, 0.0).T
    base_s[...] = base
    lane = lax.broadcasted_iota(jnp.int32, (1, 128), 1)
    within = lane % 64
    half = [slice(0, 64), slice(64, 128)]
    mine = [lane < 64, lane >= 64]
    qt_s[...] = (qh[...].astype(F32) * 0.125).T.astype(BF16)
    for h in range(2):
        gap = jnp.full((1, 128), bias[0, 2 * y + h] - bias[1, 2 * y + h], F32)
        hi = gap.astype(BF16).astype(F32)
        mid = (gap - hi).astype(BF16).astype(F32)
        low = gap - hi - mid
        coef = jnp.where(within < 16, MASK, jnp.where(within < 20, hi, jnp.where(within < 24, mid, low)))
        qa_s[h] = jnp.where(mine[h], qh[...].astype(F32) * 0.125, base * coef).astype(BF16)
        ka_s[h] = jnp.where(mine[h], kh[...].astype(F32), base).astype(BF16)
    def scores(i, carry):
        rows = span(i, BQ)
        for h in range(2):
            s = lax.dot_general(qa_s[h, rows, :], ka_s[h], (((1,), (1,)), ((), ())),
                                preferred_element_type=F32)
            top = jnp.max(s, axis=1, keepdims=True)
            eb_s[h, rows, :] = jnp.exp(s - top).astype(BF16)
        return carry

    lax.fori_loop(0, ROW // BQ, scores, 0)
    for e in (0,) + ORDER:
        to_sibling(e)
    for cp in ins[2]:
        cp.wait()
    for h in range(2):
        va_s[h] = jnp.where(mine[h], vh[...].astype(F32), 1.0).astype(BF16)

    def forward(i, carry):
        rows = span(i, BQ)
        un = [jnp.dot(eb_s[h, rows, :], va_s[h], preferred_element_type=F32) for h in range(2)]
        inv = 1.0 / pltpu.roll(jnp.where(mine[0], un[1], un[0]), 64, 1)
        mix = jnp.where(mine[0], un[0], un[1]) * inv
        inv_s[rows, :] = inv
        c_s32[rows, :] = mix
        ctxh[rows, :] = mix.astype(BF16)
        return carry

    lax.fori_loop(0, ROW // BQ, forward, 0)
    back = [unspread(ctxh, ctx, a_s.at[4], a_r.at[4], a_l.at[4])]

    for cp in siblings:
        cp.wait()
    dm_copy.wait()
    for xi in range(NX):
        rows = wf[xi].reshape(256, D)
        got = lax.dot_general(dm[...], rows, (((1,), (1,)), ((), ())), preferred_element_type=F32)
        dctx[:, 256 * xi:256 * (xi + 1)] = got.astype(BF16)
    ins.append(spread(dctx, dh, a_s.at[3], a_r.at[3], a_l.at[3]))

    for cp in back[0]:
        cp.wait()
    for xi in range(NX):
        part = ctx[:, 256 * xi:256 * (xi + 1)].astype(F32).T.astype(BF16)
        got = jnp.dot(part, dm[...], preferred_element_type=F32)
        g[xi] = got.astype(BF16).reshape(8, 2, 16, D)
    sibs = {}
    for off in LATE:
        zt = lax.rem(z + off, NZ)
        cp = remote(g.at[:, zt, sib], sa.at[:, zt], c_s.at[off], c_r.at[off], core=sib)
        cp.start()
        sibs[off] = cp

    xcp, zcp = {}, []

    def sum_cores(off):
        zt = lax.rem(z + off, NZ)
        sibs[off].wait()
        val = g[:, zt, c].astype(F32) + sa[:, zt].astype(F32)
        hf[off] = val
        hs[off] = val.astype(BF16)
        for d in range(1, NX):
            to = lax.rem(x + d, NX)
            cp = remote(hs.at[off, to], hr.at[off, d], x_s.at[off, d], x_r.at[off, d], x=to)
            cp.start()
            xcp[off, d] = cp

    ins[3][-1].wait()

    def queries_grad(n, carry):
        pair = []
        for m in range(2):
            at = 2 * n + m
            odd = at % 2
            d = odd * ((at + 1) // 2) + (1 - odd) * ((NY - at // 2) % NY)
            to = lax.rem(y + d, NY)
            cp = remote(dctx.at[:, span(to)], dh.at[span(y), :], a_s.at[3, d], a_r.at[3, d], ctx=to)
            if m:
                cp.wait()
            else:
                pl.when(n > 0)(cp.wait)
            pair.append(span(lax.rem(y + NY - d, NY)))

        def both(ref, *lead):
            return jnp.concatenate([ref[(*lead, r, slice(None))] for r in pair], axis=0)

        def keep(ref, val, *lead):
            for m in range(2):
                ref[(*lead, pair[m], slice(None))] = val[128 * m:128 * (m + 1)]

        dn = (both(dh).astype(F32) * both(inv_s)).astype(BF16)
        keep(dn_s, dn)
        dnf = dn.astype(F32)
        prod = dnf * both(c_s32)
        o_blk = both(base_s)
        outs, sums = [], []
        for h in range(2):
            delta = jnp.sum(jnp.where(mine[h], prod, 0.0), axis=1, keepdims=True)
            hi = delta.astype(BF16).astype(F32)
            mid = (delta - hi).astype(BF16).astype(F32)
            low = delta - hi - mid
            da = jnp.where(within == 0, -hi, jnp.where(within == 1, -mid, jnp.where(within == 2, -low, 0.0)))
            da = jnp.where(mine[h], dnf, da).astype(BF16)
            t = lax.dot_general(da, va_s[h], (((1,), (1,)), ((), ())), preferred_element_type=F32)
            ds = (both(eb_s, h).astype(F32) * t).astype(BF16)
            keep(ds_s, ds, h)
            got = jnp.dot(ds, ka_s[h], preferred_element_type=F32)
            u = jnp.where(mine[1 - h] & (within >= 16) & (within < 20), got, 0.0)
            sums.append(jnp.sum(u * o_blk, axis=0, keepdims=True))
            sums.append(jnp.sum(u * (1.0 - o_blk), axis=0, keepdims=True))
            outs.append(got)
        keep(dqh, (jnp.where(mine[0], outs[0], outs[1]) * 0.125).astype(BF16))
        return tuple(a + b for a, b in zip(carry, sums))

    zero = jnp.zeros((1, 128), F32)
    sums = lax.fori_loop(0, 2, queries_grad, (zero,) * 4)
    for off in LATE[:4]:
        sum_cores(off)
    sums = lax.fori_loop(2, 4, queries_grad, sums)
    back.append(unspread(dqh, dq, a_s.at[6], a_r.at[6], a_l.at[6]))
    for off in LATE[4:]:
        sum_cores(off)
    dnt_s[...] = dn_s[...].astype(F32).T.astype(BF16)

    def values_grad(j, carry):
        cols = span(j, 256)
        for h in range(2):
            dvt[half[h], :] = jnp.dot(dnt_s[half[h], :], eb_s[h, :, cols], preferred_element_type=F32)
        dvh[cols, :] = dvt[...].T.astype(BF16)
        return carry

    lax.fori_loop(0, ROW // 256, values_grad, 0)
    back.append(unspread(dvh, dv, a_s.at[5], a_r.at[5], a_l.at[5]))
    total = [jnp.sum(a, axis=1, keepdims=True) for a in sums]
    row = lax.broadcasted_iota(jnp.int32, (8, 128), 0)
    col = lax.broadcasted_iota(jnp.int32, (8, 128), 1) - 2 * y
    tile = jnp.zeros((8, 128), F32)
    for h in range(2):
        for r in range(2):
            tile = jnp.where((row == r) & (col == h), total[2 * h + r], tile)
    bs[3] = tile
    bsib = remote(bs.at[3], br.at[0], b_s.at[0], b_r.at[0], core=sib)
    bsib.start()

    def keys_grad(j, carry):
        cols = span(j, 256)
        for h in range(2):
            dkt[half[h], :] = jnp.dot(qt_s[half[h], :], ds_s[h, :, cols], preferred_element_type=F32)
        dkh[cols, :] = dkt[...].T.astype(BF16)
        return carry

    lax.fori_loop(0, ROW // 256, keys_grad, 0)
    back.append(unspread(dkh, dk, a_s.at[7], a_r.at[7], a_l.at[7]))

    for n in range(4):
        cols = slice(256 * n, 256 * (n + 1))
        got = jnp.dot(ctx[...], wf[...].reshape(D, D)[:, cols], preferred_element_type=F32)
        mixed[:, cols] = got.astype(BF16)
    mixed_copy = pltpu.make_async_copy(mixed, mixed_o, w_l.at[0])
    mixed_copy.start()
    bsib.wait()
    bs[0] = bs[3] + br[0]
    bz = []
    for d in range(1, NZ):
        cp = remote(bs.at[0], br.at[d], b_s.at[d], b_r.at[d], z=lax.rem(z + d, NZ))
        cp.start()
        bz.append(cp)

    for off in LATE:
        for d in range(1, NX):
            xcp[off, d].wait()
        val = hf[off, x] + hr[off, 1].astype(F32) + hr[off, 2].astype(F32) + hr[off, 3].astype(F32)
        if off:
            zs[off] = val.astype(BF16)
            cp = remote(zs.at[off], zr.at[off], z_s.at[off], z_r.at[off], z=lax.rem(z + off, NZ))
            cp.start()
            zcp.append(cp)
        if off == 4:
            for cp in bz:
                cp.wait()
            tile = bs[0]
            for d in range(1, NZ):
                tile = tile + br[d]
            bs[1] = tile
            bx = []
            for d in range(1, NX):
                cp = remote(bs.at[1], br.at[7 + d], b_s.at[7 + d], b_r.at[7 + d], x=lax.rem(x + d, NX))
                cp.start()
                bx.append(cp)
    for cp in bx:
        cp.wait()
    bs[2] = bs[1] + br[8] + br[9] + br[10]
    by = []
    for d in range(1, NY):
        cp = remote(bs.at[2], br.at[10 + d], b_s.at[10 + d], b_r.at[10 + d], ctx=lax.rem(y + d, NY))
        cp.start()
        by.append(cp)
    for cp in zcp:
        cp.wait()
    for d in range(1, NZ):
        val = val + zr[d].astype(F32)
    ys[...] = val.astype(BF16)
    ycp = []
    for d in ORDER:
        cp = remote(ys, yr.at[d], y_s.at[d], y_r.at[d], ctx=lax.rem(y + d, NY))
        cp.start()
        ycp.append(cp)
    for cp in by:
        cp.wait()
    tile = bs[2]
    for d in range(1, NY):
        tile = tile + br[10 + d]
    bg[...] = tile
    for cp in back[1] + back[2] + back[3] + [mixed_copy]:
        cp.wait()
    for n, d in enumerate(ORDER):
        ycp[n].wait()
        val = val + yr[d].astype(F32)
    wg[...] = val


def finish_kernel(*refs):
    for src, dst in zip(refs[:6], refs[6:]):
        dst[...] = src[:dst.shape[0], :dst.shape[1]]


VM = pl.BlockSpec(memory_space=pltpu.VMEM)
SM = pl.BlockSpec(memory_space=pltpu.SMEM)
ANY = pl.BlockSpec(memory_space=pl.ANY)
DMA = pltpu.SemaphoreType.DMA
LIMIT = 62 * 1024 * 1024


def sds(shape, dtype):
    return jax.ShapeDtypeStruct(shape, dtype)


def on_device(queries, keys, values, d_mixed, series_ids, variate_ids, variate_bias, w_out):
    tokens = sds((TOK, D), BF16)
    wide = pltpu.VMEM((ROW, 128), BF16)
    wide32 = pltpu.VMEM((ROW, 128), F32)
    pair = pltpu.VMEM((2, ROW, 128), BF16)
    square = pltpu.VMEM((2, ROW, ROW), BF16)
    results = pl.pallas_call(
        fused_kernel,
        out_shape=[tokens] * 4 + [sds((16, D), F32), sds((8, 128), F32)],
        in_specs=[ANY] * 7 + [SM],
        out_specs=[ANY] * 4 + [VM] * 2,
        scratch_shapes=[
            pltpu.VMEM((TOK, D), BF16), pltpu.VMEM((TOK, D), BF16),
            wide, wide, wide, wide,
            pltpu.VMEM((1, ROW), jnp.int32), pltpu.VMEM((1, ROW), jnp.int32),
            pltpu.VMEM((NX, NZ, NC, 16, D), BF16), pltpu.VMEM((TOK, D), BF16),
            wide32, pair, pair, pair, pltpu.VMEM((128, ROW), BF16),
            square, square, wide32, wide32, wide, pltpu.VMEM((128, ROW), BF16),
            pltpu.VMEM((128, 256), F32), pltpu.VMEM((128, 256), F32),
            wide, wide, wide, wide,
            pltpu.VMEM((TOK, D), BF16),
            pltpu.VMEM((NX, NZ, NC, 16, D), BF16), pltpu.VMEM((NX, NZ, 16, D), BF16),
            pltpu.VMEM((8, NX, 16, D), BF16), pltpu.VMEM((8, NX, 16, D), F32), pltpu.VMEM((8, NX, 16, D), BF16),
            pltpu.VMEM((8, 16, D), BF16), pltpu.VMEM((8, 16, D), BF16),
            pltpu.VMEM((16, D), BF16), pltpu.VMEM((8, 16, D), BF16),
            pltpu.VMEM((4, 8, 128), F32), pltpu.VMEM((18, 8, 128), F32),
            DMA((8, 8)), DMA((8, 8)), DMA((8,)),
            DMA((2, 8)), DMA((2, 8)), DMA((2,)),
            DMA((8,)), DMA((8,)),
            DMA((8, 4)), DMA((8, 4)),
            DMA((8,)), DMA((8,)), DMA((2,)),
            DMA((8,)), DMA((8,)),
            DMA((8, 4)), DMA((8, 4)),
            DMA((8,)), DMA((8,)),
            DMA((8,)), DMA((8,)),
            DMA((18,)), DMA((18,)),
        ],
        compiler_params=pltpu.CompilerParams(collective_id=0, has_side_effects=True, vmem_limit_bytes=LIMIT),
        name="fused",
    )(queries[0], keys[0], values[0], d_mixed[0], series_ids, variate_ids, w_out, variate_bias)
    mixed, dq, dk, dv, wg, bg = pl.pallas_call(
        finish_kernel,
        out_shape=[tokens] * 4 + [sds((16, D), F32), sds((2, HEADS), F32)],
        in_specs=[VM] * 6,
        out_specs=[VM] * 6,
        compiler_params=pltpu.CompilerParams(vmem_limit_bytes=LIMIT),
        name="finish",
    )(*results)
    return mixed[None], dq[None], dk[None], dv[None], wg, bg


def solution(mesh):
    finer = Mesh(mesh.devices.reshape(NY, NX, NZ, NC), ("ctx", "x", "z", "core"))
    tokens = P(DP, "ctx", None)
    ids = P(DP, "ctx")
    return jax.shard_map(
        on_device,
        mesh=finer,
        in_specs=(tokens, tokens, tokens, tokens, ids, ids, P(), P(DP, None)),
        out_specs=(tokens, tokens, tokens, tokens, P(DP, None), P()),
        check_vma=False,
    )
```

time: 93.2 us -> 83.9 us (0.900)
  the two profiles are of different devices: /device:TPU:8 before, /device:TPU:1 now
where the time goes in v3:
time: 83.9 us; the launch traced here: 83.8 us
  Pallas kernels  83.1 us (99%)
    pallas_call x1, Pallas kernels, on_device(): pl.pallas_call(fused_kernel, out_shape=[tokens] * 4 + [sds((16, D), F32),...  80.9 us
    pallas_call x1, Pallas kernels, on_device(): pl.pallas_call(finish_kernel, out_shape=[tokens] * 4 + [sds((16, D), F32)...  2.19 us

profile of v3, /device:TPU:1, one launch (start us, length us, event | category | flops | bytes accessed | tf_op | source)
XLA Modules:
  0.0 83.8 jit_solution(11050786816160162693)
XLA Ops:
  0.6 80.9 %fused.1 = (bf16[128,1024]{1,0:T(8,128)(2,1)}, bf16[128,1024]{1,0:T(8,128)(2,1)}, bf16[128,1024]{1,0:T(8,128)(2,1)}, bf16[128,1024]{1,0:T(8,128)(2,1)}, f32[16,1024]{1,0:T(8,128)}, /*index=5*/f32[8,128]{1,0:T(8,128)}) custom-call(bf16[128,1024]{1,0:T(8,128)(2,1)} %bitcast.8, bf16[128,1024]{1,0:T(8,128)(2,1)} %bitcast.9, bf16[128,1024]{1,0:T(8,128)(2,1)} %bitcast.10, ...), custom_call_target="tpu_custom_call" | custom-call | tf_op jit(solution)/shard_map/fused/pallas_call | solution.py:398
  81.6 2.2 %finish.1 = (bf16[128,1024]{1,0:T(8,128)(2,1)}, bf16[128,1024]{1,0:T(8,128)(2,1)}, bf16[128,1024]{1,0:T(8,128)(2,1)}, bf16[128,1024]{1,0:T(8,128)(2,1)}, f32[16,1024]{1,0:T(8,128)}, /*index=5*/f32[2,16]{1,0:T(2,128)}) custom-call(bf16[128,1024]{1,0:T(8,128)(2,1)} %get-tuple-element.18.refs_0_, bf16[128,1024]{1,0:T(8,128)(2,1)} %get-tuple-element.19.refs_1_, ...), custom_call_target="tpu_custom_call" | custom-call | tf_op jit(solution)/shard_map/finish/pallas_call | solution.py:432

commit v4 on v3

--- a/solution.py
+++ b/solution.py
@@ -105,17 +105,21 @@
             from_x[e, d] = cp
 
     to_x(0)
-    ids = []
-    for n, (src, dst) in enumerate(((ser, ser_o), (var, var_o))):
-        for d in ORDER:
-            cp = remote(src, dst.at[:, span(y)], i_s.at[n, d], i_r.at[n, d], ctx=lax.rem(y + d, NY))
+    ids, ins = [], []
+
+    def send_ids():
+        for n, (src, dst) in enumerate(((ser, ser_o), (var, var_o))):
+            for d in ORDER:
+                cp = remote(src, dst.at[:, span(y)], i_s.at[n, d], i_r.at[n, d], ctx=lax.rem(y + d, NY))
+                cp.start()
+                ids.append(cp)
+            cp = pltpu.make_async_copy(src, dst.at[:, span(y)], i_l.at[n])
             cp.start()
             ids.append(cp)
-        cp = pltpu.make_async_copy(src, dst.at[:, span(y)], i_l.at[n])
-        cp.start()
-        ids.append(cp)
-    ins = []
+
     for n, (src, dst) in enumerate(((q, qh), (k, kh), (v, vh))):
+        if n == 2:
+            send_ids()
         ins.append(spread(src, dst, a_s.at[n], a_r.at[n], a_l.at[n]))
 
     own.wait()
@@ -267,12 +271,9 @@
         return tuple(a + b for a, b in zip(carry, sums))
 
     zero = jnp.zeros((1, 128), F32)
-    sums = lax.fori_loop(0, 2, queries_grad, (zero,) * 4)
-    for off in LATE[:4]:
-        sum_cores(off)
-    sums = lax.fori_loop(2, 4, queries_grad, sums)
+    sums = lax.fori_loop(0, 4, queries_grad, (zero,) * 4)
     back.append(unspread(dqh, dq, a_s.at[6], a_r.at[6], a_l.at[6]))
-    for off in LATE[4:]:
+    for off in LATE:
         sum_cores(off)
     dnt_s[...] = dn_s[...].astype(F32).T.astype(BF16)
 

time: 83.9 us -> 82.5 us (0.983)
  Pallas kernels: 83.1 us -> 81 us
    pallas_call x1, Pallas kernels: 80.9 us -> 78.8 us  [on_device(): pl.pallas_call(fused_kernel, out_shape=[tokens] * 4 + [sds((16, D), F32),...]
where the time goes in v4:
time: 82.5 us; the launch traced here: 81.6 us
  Pallas kernels  81 us (98%)
    pallas_call x1, Pallas kernels, on_device(): pl.pallas_call(fused_kernel, out_shape=[tokens] * 4 + [sds((16, D), F32),...  78.8 us
    pallas_call x1, Pallas kernels, on_device(): pl.pallas_call(finish_kernel, out_shape=[tokens] * 4 + [sds((16, D), F32)...  2.19 us

profile of v4, /device:TPU:1, one launch (start us, length us, event | category | flops | bytes accessed | tf_op | source)
XLA Modules:
  0.0 81.6 jit_solution(17673544631916086803)
XLA Ops:
  0.6 78.8 %fused.1 = (bf16[128,1024]{1,0:T(8,128)(2,1)}, bf16[128,1024]{1,0:T(8,128)(2,1)}, bf16[128,1024]{1,0:T(8,128)(2,1)}, bf16[128,1024]{1,0:T(8,128)(2,1)}, f32[16,1024]{1,0:T(8,128)}, /*index=5*/f32[8,128]{1,0:T(8,128)}) custom-call(bf16[128,1024]{1,0:T(8,128)(2,1)} %bitcast.8, bf16[128,1024]{1,0:T(8,128)(2,1)} %bitcast.9, bf16[128,1024]{1,0:T(8,128)(2,1)} %bitcast.10, ...), custom_call_target="tpu_custom_call" | custom-call | tf_op jit(solution)/shard_map/fused/pallas_call | solution.py:399
  79.4 2.2 %finish.1 = (bf16[128,1024]{1,0:T(8,128)(2,1)}, bf16[128,1024]{1,0:T(8,128)(2,1)}, bf16[128,1024]{1,0:T(8,128)(2,1)}, bf16[128,1024]{1,0:T(8,128)(2,1)}, f32[16,1024]{1,0:T(8,128)}, /*index=5*/f32[2,16]{1,0:T(2,128)}) custom-call(bf16[128,1024]{1,0:T(8,128)(2,1)} %get-tuple-element.18.refs_0_, bf16[128,1024]{1,0:T(8,128)(2,1)} %get-tuple-element.19.refs_1_, ...), custom_call_target="tpu_custom_call" | custom-call | tf_op jit(solution)/shard_map/finish/pallas_call | solution.py:433

commit v5 on v4

--- a/solution.py
+++ b/solution.py
@@ -91,6 +91,7 @@
     own.start()
     meet(others("ctx", NY) + others("x", NX) + others("z", NZ) + [{"core": sib}])
 
+    ins = [spread(q, qh, a_s.at[0], a_r.at[0], a_l.at[0])]
     from_z, from_x = {}, {}
     for d in ORDER:
         cp = remote(w, wf.at[x, z, c], wz_s.at[d], wz_r.at[d], z=lax.rem(z + d, NZ))
@@ -105,7 +106,7 @@
             from_x[e, d] = cp
 
     to_x(0)
-    ids, ins = [], []
+    ids = []
 
     def send_ids():
         for n, (src, dst) in enumerate(((ser, ser_o), (var, var_o))):
@@ -117,7 +118,7 @@
             cp.start()
             ids.append(cp)
 
-    for n, (src, dst) in enumerate(((q, qh), (k, kh), (v, vh))):
+    for n, (src, dst) in ((1, (k, kh)), (2, (v, vh))):
         if n == 2:
             send_ids()
         ins.append(spread(src, dst, a_s.at[n], a_r.at[n], a_l.at[n]))

time: 82.5 us -> 82.5 us (level)
  no operation moved by 1% of the time
where the time goes in v5:
time: 82.5 us; the launch traced here: 81.6 us
  Pallas kernels  81 us (98%)
    pallas_call x1, Pallas kernels, on_device(): pl.pallas_call(fused_kernel, out_shape=[tokens] * 4 + [sds((16, D), F32),...  78.8 us
    pallas_call x1, Pallas kernels, on_device(): pl.pallas_call(finish_kernel, out_shape=[tokens] * 4 + [sds((16, D), F32)...  2.19 us

profile of v5, /device:TPU:1, one launch (start us, length us, event | category | flops | bytes accessed | tf_op | source)
XLA Modules:
  0.0 81.6 jit_solution(6739659162890417649)
XLA Ops:
  0.6 78.8 %fused.1 = (bf16[128,1024]{1,0:T(8,128)(2,1)}, bf16[128,1024]{1,0:T(8,128)(2,1)}, bf16[128,1024]{1,0:T(8,128)(2,1)}, bf16[128,1024]{1,0:T(8,128)(2,1)}, f32[16,1024]{1,0:T(8,128)}, /*index=5*/f32[8,128]{1,0:T(8,128)}) custom-call(bf16[128,1024]{1,0:T(8,128)(2,1)} %bitcast.8, bf16[128,1024]{1,0:T(8,128)(2,1)} %bitcast.9, bf16[128,1024]{1,0:T(8,128)(2,1)} %bitcast.10, ...), custom_call_target="tpu_custom_call" | custom-call | tf_op jit(solution)/shard_map/fused/pallas_call | solution.py:400
  79.4 2.2 %finish.1 = (bf16[128,1024]{1,0:T(8,128)(2,1)}, bf16[128,1024]{1,0:T(8,128)(2,1)}, bf16[128,1024]{1,0:T(8,128)(2,1)}, bf16[128,1024]{1,0:T(8,128)(2,1)}, f32[16,1024]{1,0:T(8,128)}, /*index=5*/f32[2,16]{1,0:T(2,128)}) custom-call(bf16[128,1024]{1,0:T(8,128)(2,1)} %get-tuple-element.18.refs_0_, bf16[128,1024]{1,0:T(8,128)(2,1)} %get-tuple-element.19.refs_1_, ...), custom_call_target="tpu_custom_call" | custom-call | tf_op jit(solution)/shard_map/finish/pallas_call | solution.py:434
